TPU v7x, 256 devices: a whole 4x4x8 slice. The times are simulated.
256 devices in a mesh: gx: 8 (over y, core), gy: 8 (over x, z_lo), gz: 4 (over z_hi).
Axes of the slice: x: 4, y: 4, z: 8 (z_hi: 4, z_lo: 2; z = z_hi * 2 + z_lo), core: 2. Of those that a mesh axis runs over, the one named last changes fastest.
Arguments:
- rhs: float32 [8, 8, 3, 162, 1024], P('gx', 'gy', None, None, 'gz'), may hold values from -6 to 6
- angles: float32 [8, 8, 3, 1024], P('gx', 'gy', None, 'gz'), may hold values from -3.140625 to 3.140625
- self_mob: float32 [486, 486], replicated, may hold values from -0.25 to 0.25
- near_mat: float32 [486, 486], replicated, may hold values from -0.25 to 0.25
- near_weight: float32 [8, 8, 8, 1024], P('gx', 'gy', None, 'gz'), may hold values from -2 to 2
- neighbours: int32 [8, 8, 8, 1024], P('gx', 'gy', None, 'gz'), may hold values from 0 to 2111, as said below
- cells: int32 [8, 8, 1024], P('gx', 'gy', 'gz'), may hold values from 0 to 191
- blob_weight: float32 [162], replicated, may hold values from -0.5 to 0.5
- skel_perm: int32 [2, 384], replicated, may hold values from 0 to 383, each once within a row
- interp: float32 [2, 192, 192], replicated, may hold values from -0.4375 to 0.4375
- sibling_ops: float32 [2, 192, 192], replicated, may hold values from -0.375 to 0.375
- root_op: float32 [192, 192], replicated, may hold values from -0.0625 to 0.0625
Outputs:
- solution: float32 [8, 8, 3, 162, 1024], P('gx', 'gy', None, None, 'gz')
- lsq_residual: float32 [], replicated
Inputs may be any that keep to these rules, and one draw needn't show every extreme that they name: `neighbours`: each id is s * 256 + j with slot s in 0..8 and j < 256; j < 64 whenever s != 4, and some id in every draw reaches j = 63 in slot 8.
All inputs are finite; a program needn't handle non-finite values.
Results may differ from a plain program's by a relative error of at most 0.0003.
Values sent between devices are 32-bit elements; how exact they have to be, the bound alone decides.
A program may use at most 128 MiB of HBM per device.

v0:
```python
import jax
import jax.numpy as jnp
from jax import lax
from jax.sharding import PartitionSpec as P

highest = lax.Precision.HIGHEST
epsilon = 1e-06


def padded(shard, sides, width):
    for axis, dim in sides:
        size, length = (lax.axis_size(axis), shard.shape[dim])
        up = [(i, (i + 1) % size) for i in range(size)]
        down = [(j, i) for i, j in up]
        last = lax.slice_in_dim(shard, length - width, length, axis=dim)
        leading = lax.slice_in_dim(shard, 0, width, axis=dim)
        before = lax.ppermute(last, axis, up)
        after = lax.ppermute(leading, axis, down)
        shard = jnp.concatenate([before, shard, after], axis=dim)
    return shard


def from_partner(value, axis, stride):
    mask = 2**stride
    pairs = [(source, source ^ mask) for source in range(lax.axis_size(axis))]
    return lax.ppermute(value, axis, pairs)


def frame(angles):
    cos_yaw = jnp.cos(angles[0])
    sin_yaw = jnp.sin(angles[0])
    cos_pitch = jnp.cos(angles[1])
    sin_pitch = jnp.sin(angles[1])
    cos_roll = jnp.cos(angles[2])
    sin_roll = jnp.sin(angles[2])
    return (
        (
            cos_yaw * cos_pitch,
            cos_yaw * sin_pitch * sin_roll - sin_yaw * cos_roll,
            cos_yaw * sin_pitch * cos_roll + sin_yaw * sin_roll,
        ),
        (
            sin_yaw * cos_pitch,
            sin_yaw * sin_pitch * sin_roll + cos_yaw * cos_roll,
            sin_yaw * sin_pitch * cos_roll - cos_yaw * sin_roll,
        ),
        (-sin_pitch, cos_pitch * sin_roll, cos_pitch * cos_roll),
    )


def rotate(source, rotation, inverse):
    components = []
    for target_axis in range(3):
        summed = jnp.zeros_like(source[0])
        for source_axis in range(3):
            factor = (
                rotation[source_axis][target_axis]
                if inverse
                else rotation[target_axis][source_axis]
            )
            summed = summed + factor[None, :] * source[source_axis]
        components.append(summed)
    return jnp.stack(components)


def least_squares(beta, diag_first, below_first, above_second, diag_second, below_second):
    first_norm = jnp.sqrt(diag_first * diag_first + below_first * below_first)
    first_cos = diag_first / first_norm
    first_sin = below_first / first_norm
    top_right = first_cos * above_second + first_sin * diag_second
    lower_right = first_cos * diag_second - first_sin * above_second
    second_norm = jnp.sqrt(lower_right * lower_right + below_second * below_second)
    second_cos = lower_right / second_norm
    second_sin = below_second / second_norm
    carried = -first_sin * beta
    coef_two = second_cos * carried / second_norm
    coef_one = (first_cos * beta - top_right * coef_two) / first_norm
    return (coef_one, coef_two, jnp.abs(second_sin * carried))


def contract_last(left, right):
    return lax.dot_general(left, right, (((1,), (1,)), ((), ())), precision=highest)


def body(
    rhs,
    angles,
    self_mob,
    near_mat,
    near_weight,
    neighbours,
    cells,
    blob_weight,
    skel_perm,
    interp,
    sibling_ops,
    root_op,
):
    blob_count = blob_weight.shape[0]
    dof_count = 3 * blob_count
    box_bodies = rhs.shape[-1]
    skel_points = root_op.shape[0]
    level_count = skel_perm.shape[0]
    initial = rhs.reshape(3, blob_count, box_bodies)
    rotation = frame(angles.reshape(3, box_bodies))
    near_coef = near_weight.reshape(-1, box_bodies)
    link_ids = neighbours.reshape(-1, box_bodies)
    box_slot = link_ids // box_bodies
    body_slot = link_ids % box_bodies
    is_own = (box_slot == 4)[:, :, None]
    occupancy = (
        cells.reshape(box_bodies)[:, None] == jnp.arange(skel_points, dtype=jnp.int32)[None, :]
    ).astype(jnp.float32)
    permuter = (
        skel_perm[:, :, None] == jnp.arange(2 * skel_points, dtype=jnp.int32)[None, None, :]
    ).astype(jnp.float32)
    layer_index = lax.axis_index("gz")

    def operate(source):
        turned = rotate(source, rotation, False).reshape(dof_count, box_bodies)
        mixture = jnp.dot(self_mob, turned, precision=highest).reshape(3, blob_count, box_bodies)
        own_part = source + rotate(mixture, rotation, True)
        ghosts = padded(source[None, None], (("gx", 0), ("gy", 1)), 1)
        ghost_width = ghosts.shape[-1]
        ghost_boxes = ghosts.reshape(9, dof_count, ghost_width)
        own_rows = source.reshape(dof_count, box_bodies).T
        gathered = jnp.zeros((box_bodies, dof_count), jnp.float32)
        for link_index in range(near_coef.shape[0]):
            remote = ghost_boxes[
                box_slot[link_index], :, jnp.minimum(body_slot[link_index], ghost_width - 1)
            ]
            own_value = own_rows[body_slot[link_index]]
            gathered = gathered + near_coef[link_index][:, None] * jnp.where(
                is_own[link_index], own_value, remote
            )
        near_part = contract_last(near_mat, gathered).reshape(3, blob_count, box_bodies)
        moments = jnp.einsum("cqn,q->cn", source, blob_weight, precision=highest)
        charges = jnp.dot(moments, occupancy, precision=highest)
        partners = []
        high_flags = []
        for tree_level in range(level_count):
            partner = from_partner(charges, "gz", tree_level)
            high_side = layer_index >> tree_level & 1 == 1
            low_child = jnp.where(high_side, partner, charges)
            higher = jnp.where(high_side, charges, partner)
            joined = jnp.concatenate([low_child, higher], axis=1)
            picked = contract_last(joined, permuter[tree_level])
            charges = picked[:, :skel_points] + jnp.dot(
                picked[:, skel_points:], interp[tree_level], precision=highest
            )
            partners.append(partner)
            high_flags.append(high_side)
        root_total = lax.psum(charges, ("gx", "gy"))
        potential = jnp.dot(root_total - charges, root_op, precision=highest)
        for tree_level in reversed(range(level_count)):
            spread = jnp.concatenate(
                [potential, contract_last(potential, interp[tree_level])], axis=1
            )
            placed = jnp.dot(spread, permuter[tree_level], precision=highest)
            child_part = jnp.where(
                high_flags[tree_level], placed[:, skel_points:], placed[:, :skel_points]
            )
            potential = child_part + jnp.dot(
                partners[tree_level], sibling_ops[tree_level], precision=highest
            )
        body_values = contract_last(potential, occupancy)
        far_part = blob_weight[None, :, None] * body_values[:, None, :]
        return own_part + near_part + far_part

    def global_sum(value):
        return lax.psum(value, ("gx", "gy", "gz"))

    beta = jnp.sqrt(global_sum(jnp.sum(initial * initial)) + epsilon)
    basis_one = initial / beta
    image_one = operate(basis_one)
    diag_first = global_sum(jnp.sum(image_one * basis_one))
    residue_one = image_one - diag_first * basis_one
    below_first = jnp.sqrt(global_sum(jnp.sum(residue_one * residue_one)) + epsilon)
    basis_two = residue_one / below_first
    image_two = operate(basis_two)
    above_second, diag_second = lax.psum(
        (jnp.sum(image_two * basis_one), jnp.sum(image_two * basis_two)), ("gx", "gy", "gz")
    )
    residue_two = image_two - above_second * basis_one - diag_second * basis_two
    below_second = jnp.sqrt(global_sum(jnp.sum(residue_two * residue_two)) + epsilon)
    coef_one, coef_two, lsq_residual = least_squares(
        beta, diag_first, below_first, above_second, diag_second, below_second
    )
    result = coef_one * basis_one + coef_two * basis_two
    return (result[None, None], lsq_residual)


def solution(mesh):
    in_specs = (
        P("gx", "gy", None, None, "gz"),
        P("gx", "gy", None, "gz"),
        P(),
        P(),
        P("gx", "gy", None, "gz"),
        P("gx", "gy", None, "gz"),
        P("gx", "gy", "gz"),
        P(),
        P(),
        P(),
        P(),
        P(),
    )
    out_specs = (P("gx", "gy", None, None, "gz"), P())
    return jax.shard_map(body, mesh=mesh, in_specs=in_specs, out_specs=out_specs, check_vma=False)
```

profile of v0, /device:TPU:1, one launch (start us, length us, event | category | flops | bytes accessed | tf_op | source)
XLA Modules:
  0.0 992.4 jit_solution(14893652054346004471)
XLA Ops:
  3.5 81.4 %psum.56 = f32[]{:T(128)} all-reduce(f32[]{:T(128)} %multiply_reduce_fusion.5), channel_id=1, replica_groups=mesh['gx'=8,'gy'=8,'gz'=4] {'gx','gy','gz'}, use_global_device_ids=true, to_apply=%region_1.2 | all-reduce | flops 1 | bytes 8 | tf_op jit(solution)/shard_map/psum | solution.py:171
  118.9 133.0 %psum.57 = f32[3,192]{1,0:T(4,128)S(1)} all-reduce(f32[3,192]{1,0:T(4,128)S(1)} %slice_add_fusion.2), channel_id=1, replica_groups=mesh['gx'=8,'gy'=8,'gz'=4] {'gx','gy'}, use_global_device_ids=true, to_apply=%region_2.3 | all-reduce | flops 576 | bytes 4608 | tf_op jit(solution)/shard_map/psum | solution.py:153
  256.3 3.6 collective-permute-start.3
  262.7 18.3 %collective-permute-done.2 = f32[3,1,3,162,256]{4,1,3,2,0:T(1,128)} collective-permute-done((f32[3,1,3,162,256]{4,1,3,2,0:T(1,128)}, f32[3,1,3,162,256]{4,1,3,2,0:T(1,128)}, u32[]{:S(2)}, u32[]{:S(2)}) %collective-permute-start.2) | collective-permute-done | bytes 1493024 | tf_op jit(solution)/shard_map/ppermute | solution.py:17
  282.5 26.2 %collective-permute-done.3 = f32[3,1,3,162,256]{4,1,3,2,0:T(1,128)} collective-permute-done((f32[3,1,3,162,256]{4,1,3,2,0:T(1,128)}, f32[3,1,3,162,256]{4,1,3,2,0:T(1,128)}, u32[]{:S(2)}, u32[]{:S(2)}) %collective-permute-start.3) | collective-permute-done | bytes 1493024 | tf_op jit(solution)/shard_map/ppermute | solution.py:18
  310.2 3.8 pad_maximum_fusion
  314.0 5.5 reshape.988
  319.5 6.3 copy.81
  325.7 3.5 gather_fusion.1
  332.7 3.5 gather_fusion.13
  336.3 3.5 gather_fusion.3
  343.3 3.5 gather_fusion.7
  346.8 3.5 gather_fusion.9
  350.3 15.8 %gather_fusion.15 = f32[256,486]{1,0:T(8,128)} fusion(f32[9,486,256]{1,2,0:T(8,128)} %copy.81, s32[256]{0:T(256)S(1)} %bitcast.288), kind=kCustom, calls=%fused_computation.15 | custom fusion | bytes 997376 | tf_op jit(solution)/shard_map/gather | solution.py:129
  366.2 6.0 multiply_reduce_fusion.4
  372.2 88.5 %psum.58 = f32[]{:T(128)} all-reduce(f32[]{:T(128)} %get-tuple-element.20), channel_id=1, replica_groups=mesh['gx'=8,'gy'=8,'gz'=4] {'gx','gy','gz'}, use_global_device_ids=true, to_apply=%region_4.5 | all-reduce | flops 1 | bytes 8 | tf_op jit(solution)/shard_map/psum | solution.py:171
  463.8 72.9 %psum.59 = f32[]{:T(128)} all-reduce(f32[]{:T(128)} %multiply_reduce_fusion.3), channel_id=1, replica_groups=mesh['gx'=8,'gy'=8,'gz'=4] {'gx','gy','gz'}, use_global_device_ids=true, to_apply=%region_6.7 | all-reduce | flops 1 | bytes 8 | tf_op jit(solution)/shard_map/psum | solution.py:171
  578.4 133.3 %psum.60 = f32[3,192]{1,0:T(4,128)S(1)} all-reduce(f32[3,192]{1,0:T(4,128)S(1)} %slice_add_fusion), channel_id=1, replica_groups=mesh['gx'=8,'gy'=8,'gz'=4] {'gx','gy'}, use_global_device_ids=true, to_apply=%region_7.8 | all-reduce | flops 576 | bytes 4608 | tf_op jit(solution)/shard_map/psum | solution.py:153
  717.0 3.6 collective-permute-start.9
  723.4 18.2 %collective-permute-done.8 = f32[3,1,3,162,256]{4,1,3,2,0:T(1,128)} collective-permute-done((f32[3,1,3,162,256]{4,1,3,2,0:T(1,128)}, f32[3,1,3,162,256]{4,1,3,2,0:T(1,128)}, u32[]{:S(2)}, u32[]{:S(2)}) %collective-permute-start.8) | collective-permute-done | bytes 1493024 | tf_op jit(solution)/shard_map/ppermute | solution.py:17
  743.1 25.8 %collective-permute-done.9 = f32[3,1,3,162,256]{4,1,3,2,0:T(1,128)} collective-permute-done((f32[3,1,3,162,256]{4,1,3,2,0:T(1,128)}, f32[3,1,3,162,256]{4,1,3,2,0:T(1,128)}, u32[]{:S(2)}, u32[]{:S(2)}) %collective-permute-start.9) | collective-permute-done | bytes 1493024 | tf_op jit(solution)/shard_map/ppermute | solution.py:18
  770.5 3.7 pad_maximum_fusion.1
  774.2 5.5 reshape.992
  779.7 6.2 copy.94
  785.9 3.5 gather_fusion.17
  789.4 3.5 gather_fusion.19
  799.9 3.5 gather_fusion.25
  807.0 3.5 gather_fusion.29
  810.5 3.7 gather_fusion.31
  814.3 6.8 multiply_reduce_fusion.2
  821.1 88.2 %all-reduce = (f32[]{:T(128)}, f32[]{:T(128)}) all-reduce(f32[]{:T(128)} %get-tuple-element.9, f32[]{:T(128)} %get-tuple-element.8), channel_id=1, replica_groups=mesh['gx'=8,'gy'=8,'gz'=4] {'gx','gy','gz'}, use_global_device_ids=true, to_apply=%region_11.12 | all-reduce | flops 2 | bytes 16 | tf_op jit(solution)/shard_map/psum | solution.py:181
  915.1 73.4 %psum.63 = f32[]{:T(128)} all-reduce(f32[]{:T(128)} %multiply_reduce_fusion), channel_id=1, replica_groups=mesh['gx'=8,'gy'=8,'gz'=4] {'gx','gy','gz'}, use_global_device_ids=true, to_apply=%region_13.14 | all-reduce | flops 1 | bytes 8 | tf_op jit(solution)/shard_map/psum | solution.py:171
  (212 shorter events, 121.2 us)
Async XLA Ops:
  0.6 365.5 %copy-start = (f32[486,486]{1,0:T(8,128)S(1)}, f32[486,486]{1,0:T(8,128)}, u32[]{:S(2)}) copy-start(f32[486,486]{1,0:T(8,128)} %param.15) | copy-start | bytes 2834356
  0.6 92.8 %copy-start.6 = (f32[486,486]{1,0:T(8,128)S(1)}, f32[486,486]{1,0:T(8,128)}, u32[]{:S(2)}) copy-start(f32[486,486]{1,0:T(8,128)} %param.14) | copy-start | bytes 2834356
  0.7 95.0 %copy-start.37 = (s32[2,384]{1,0:T(2,128)S(1)}, s32[2,384]{1,0:T(2,128)}, u32[]{:S(2)}) copy-start(s32[2,384]{1,0:T(2,128)} %param.20) | copy-start | bytes 9220
  86.7 165.3 %collective-permute-start = (f32[1,1,3,162,256]{4,3,2,1,0:T(8,128)S(1)}, f32[1,1,3,162,256]{4,3,2,1,0:T(8,128)}, u32[]{:S(2)}, u32[]{:S(2)}) collective-permute-start(f32[1,1,3,162,256]{4,3,2,1,0:T(8,128)S(1)} %copy_divide_fusion), channel_id=1, source_target_pairs={{0,32},{32,64},{64,96},{96,128},{128,160},{160,192},{192,224},{224... | collective-permute-start | bytes 1493000 | tf_op jit(solution)/shard_map/ppermute | solution.py:17
  86.7 165.3 %collective-permute-start.1 = (f32[1,1,3,162,256]{4,3,2,1,0:T(8,128)S(1)}, f32[1,1,3,162,256]{4,3,2,1,0:T(8,128)}, u32[]{:S(2)}, u32[]{:S(2)}) collective-permute-start(f32[1,1,3,162,256]{4,3,2,1,0:T(8,128)S(1)} %copy_divide_fusion), channel_id=1, source_target_pairs={{32,0},{64,32},{96,64},{128,96},{160,128},{192,160},{224,192},{0,2... | collective-permute-start | bytes 1493000 | tf_op jit(solution)/shard_map/ppermute | solution.py:18
  90.2 8.2 collective-permute-start.4
  95.9 164.9 %copy-start.13 = (pred[2,384,384]{2,1,0:T(32,128)(4,1)}, pred[2,384,384]{2,1,0:T(32,128)(4,1)S(1)}, u32[]{:S(2)}) copy-start(pred[2,384,384]{2,1,0:T(32,128)(4,1)S(1)} %iota_compare_fusion) | copy-start | bytes 884740
  96.1 16.3 %copy-start.21 = (s32[1024]{0:T(1024)}, s32[1024]{0:T(1024)S(1)}, u32[]{:S(2)}) copy-start(s32[1024]{0:T(1024)S(1)} %pad_clamp_fusion.5) | copy-start | bytes 12292
  99.7 18.5 %collective-permute-start.5 = (f32[3,192]{1,0:T(4,128)S(1)}, f32[3,192]{1,0:T(4,128)S(1)}, u32[]{:S(2)}, u32[]{:S(2)}) collective-permute-start(f32[3,192]{1,0:T(4,128)S(1)} %slice_add_fusion.3), channel_id=1, source_target_pairs={{0,2},{1,3},{2,0},{3,1},{4,6},{5,7},{6,4},{7,5},{8,10},{9,11},{10,... | collective-permute-start | bytes 6920 | tf_op jit(solution)/shard_map/ppermute | solution.py:26
  114.2 137.6 %copy-start.12 = (f32[192,192]{1,0:T(8,128)S(1)}, f32[192,192]{1,0:T(8,128)}, u32[]{:S(2)}) copy-start(f32[192,192]{1,0:T(8,128)} %param.23) | copy-start | bytes 442372
  118.2 142.3 %copy-start.10 = (f32[2,192,192]{2,1,0:T(8,128)S(1)}, f32[2,192,192]{2,1,0:T(8,128)}, u32[]{:S(2)}) copy-start(f32[2,192,192]{2,1,0:T(8,128)} %param.22) | copy-start | bytes 884740
  118.2 143.2 %copy-start.38 = (s32[1,1,256]{2,1,0:T(1,128)S(1)}, s32[1,1,256]{2,1,0:T(1,128)}, u32[]{:S(2)}) copy-start(s32[1,1,256]{2,1,0:T(1,128)} %param.18) | copy-start | bytes 3076
  256.1 24.9 %collective-permute-start.2 = (f32[3,1,3,162,256]{4,1,3,2,0:T(1,128)}, f32[3,1,3,162,256]{4,1,3,2,0:T(1,128)}, u32[]{:S(2)}, u32[]{:S(2)}) collective-permute-start(f32[3,1,3,162,256]{4,1,3,2,0:T(1,128)} %copy.77), channel_id=1, source_target_pairs={{0,4},{4,8},{8,12},{12,16},{16,20},{20,24},{24,28},{28,0},{1,5},{5... | collective-permute-start | bytes 4478984 | tf_op jit(solution)/shard_map/ppermute | solution.py:17
  256.3 52.4 %collective-permute-start.3 = (f32[3,1,3,162,256]{4,1,3,2,0:T(1,128)}, f32[3,1,3,162,256]{4,1,3,2,0:T(1,128)}, u32[]{:S(2)}, u32[]{:S(2)}) collective-permute-start(f32[3,1,3,162,256]{4,1,3,2,0:T(1,128)} %copy.77), channel_id=1, source_target_pairs={{4,0},{8,4},{12,8},{16,12},{20,16},{24,20},{28,24},{0,28},{5,1},{9... | collective-permute-start | bytes 4478984 | tf_op jit(solution)/shard_map/ppermute | solution.py:18
  346.8 19.4 %copy-start.22 = (pred[256]{0:T(512)(128)(4,1)S(1)}, pred[256]{0:T(512)(128)(4,1)}, u32[]{:S(2)}) copy-start(pred[256]{0:T(512)(128)(4,1)} %get-tuple-element.10) | copy-start | bytes 772
  346.8 19.4 %copy-start.23 = (pred[256]{0:T(512)(128)(4,1)S(1)}, pred[256]{0:T(512)(128)(4,1)}, u32[]{:S(2)}) copy-start(pred[256]{0:T(512)(128)(4,1)} %get-tuple-element.11) | copy-start | bytes 772
  346.8 19.4 %copy-start.25 = (pred[256]{0:T(512)(128)(4,1)S(1)}, pred[256]{0:T(512)(128)(4,1)}, u32[]{:S(2)}) copy-start(pred[256]{0:T(512)(128)(4,1)} %get-tuple-element.12) | copy-start | bytes 772
  346.8 19.4 %copy-start.27 = (pred[256]{0:T(512)(128)(4,1)S(1)}, pred[256]{0:T(512)(128)(4,1)}, u32[]{:S(2)}) copy-start(pred[256]{0:T(512)(128)(4,1)} %get-tuple-element.13) | copy-start | bytes 772
  346.8 19.4 %copy-start.29 = (pred[256]{0:T(512)(128)(4,1)S(1)}, pred[256]{0:T(512)(128)(4,1)}, u32[]{:S(2)}) copy-start(pred[256]{0:T(512)(128)(4,1)} %get-tuple-element.14) | copy-start | bytes 772
  346.8 19.4 %copy-start.31 = (pred[256]{0:T(512)(128)(4,1)S(1)}, pred[256]{0:T(512)(128)(4,1)}, u32[]{:S(2)}) copy-start(pred[256]{0:T(512)(128)(4,1)} %get-tuple-element.15) | copy-start | bytes 772
  346.8 19.4 %copy-start.33 = (pred[256]{0:T(512)(128)(4,1)S(1)}, pred[256]{0:T(512)(128)(4,1)}, u32[]{:S(2)}) copy-start(pred[256]{0:T(512)(128)(4,1)} %get-tuple-element.16) | copy-start | bytes 772
  346.8 19.4 %copy-start.35 = (pred[256]{0:T(512)(128)(4,1)S(1)}, pred[256]{0:T(512)(128)(4,1)}, u32[]{:S(2)}) copy-start(pred[256]{0:T(512)(128)(4,1)} %get-tuple-element.17) | copy-start | bytes 772
  366.2 171.2 %copy-start.1 = (f32[1,1,3,162,256]{4,1,3,2,0:T(1,128)S(1)}, f32[1,1,3,162,256]{4,1,3,2,0:T(1,128)}, u32[]{:S(2)}) copy-start(f32[1,1,3,162,256]{4,1,3,2,0:T(1,128)} %param.12) | copy-start | bytes 1492996
  372.2 165.2 %copy-start.4 = (f32[486,256]{1,0:T(8,128)}, f32[486,256]{1,0:T(8,128)S(1)}, u32[]{:S(2)}) copy-start(f32[486,256]{1,0:T(8,128)S(1)} %get-tuple-element.21) | copy-start | bytes 1492996
  539.5 173.4 %collective-permute-start.6 = (f32[1,1,3,162,256]{4,3,2,1,0:T(8,128)S(1)}, f32[1,1,3,162,256]{4,3,2,1,0:T(8,128)}, u32[]{:S(2)}, u32[]{:S(2)}) collective-permute-start(f32[1,1,3,162,256]{4,3,2,1,0:T(8,128)S(1)} %fusion.51), channel_id=1, source_target_pairs={{0,32},{32,64},{64,96},{96,128},{128,160},{160,192},{192,224},{224... | collective-permute-start | bytes 1493000 | tf_op jit(solution)/shard_map/ppermute | solution.py:17
  540.1 172.8 %collective-permute-start.7 = (f32[1,1,3,162,256]{4,3,2,1,0:T(8,128)S(1)}, f32[1,1,3,162,256]{4,3,2,1,0:T(8,128)}, u32[]{:S(2)}, u32[]{:S(2)}) collective-permute-start(f32[1,1,3,162,256]{4,3,2,1,0:T(8,128)S(1)} %fusion.51), channel_id=1, source_target_pairs={{32,0},{64,32},{96,64},{128,96},{160,128},{192,160},{224,192},{0,2... | collective-permute-start | bytes 1493000 | tf_op jit(solution)/shard_map/ppermute | solution.py:18
  547.8 3.4 collective-permute-start.10
  552.6 24.4 %collective-permute-start.11 = (f32[3,192]{1,0:T(4,128)S(1)}, f32[3,192]{1,0:T(4,128)S(1)}, u32[]{:S(2)}, u32[]{:S(2)}) collective-permute-start(f32[3,192]{1,0:T(4,128)S(1)} %slice_add_fusion.1), channel_id=1, source_target_pairs={{0,2},{1,3},{2,0},{3,1},{4,6},{5,7},{6,4},{7,5},{8,10},{9,11},{10,... | collective-permute-start | bytes 6920 | tf_op jit(solution)/shard_map/ppermute | solution.py:26
  573.0 148.1 %copy-start.11 = (f32[2,192,192]{2,1,0:T(8,128)S(1)}, f32[2,192,192]{2,1,0:T(8,128)}, u32[]{:S(2)}) copy-start(f32[2,192,192]{2,1,0:T(8,128)} %param.22) | copy-start | bytes 884740
  575.1 147.0 %copy-start.40 = (s32[1,1,256]{2,1,0:T(1,128)S(1)}, s32[1,1,256]{2,1,0:T(1,128)}, u32[]{:S(2)}) copy-start(s32[1,1,256]{2,1,0:T(1,128)} %param.18) | copy-start | bytes 3076
  717.0 24.6 %collective-permute-start.8 = (f32[3,1,3,162,256]{4,1,3,2,0:T(1,128)}, f32[3,1,3,162,256]{4,1,3,2,0:T(1,128)}, u32[]{:S(2)}, u32[]{:S(2)}) collective-permute-start(f32[3,1,3,162,256]{4,1,3,2,0:T(1,128)} %copy.90), channel_id=1, source_target_pairs={{0,4},{4,8},{8,12},{12,16},{16,20},{20,24},{24,28},{28,0},{1,5},{5... | collective-permute-start | bytes 4478984 | tf_op jit(solution)/shard_map/ppermute | solution.py:17
  717.0 52.0 %collective-permute-start.9 = (f32[3,1,3,162,256]{4,1,3,2,0:T(1,128)}, f32[3,1,3,162,256]{4,1,3,2,0:T(1,128)}, u32[]{:S(2)}, u32[]{:S(2)}) collective-permute-start(f32[3,1,3,162,256]{4,1,3,2,0:T(1,128)} %copy.90), channel_id=1, source_target_pairs={{4,0},{8,4},{12,8},{16,12},{20,16},{24,20},{28,24},{0,28},{5,1},{9... | collective-permute-start | bytes 4478984 | tf_op jit(solution)/shard_map/ppermute | solution.py:18
  (21 other events, 177.0 us)
where the time goes:
time: 1000 us; the launch traced here: 992 us
  blocking collectives  671 us (67%)
  local copies, waits for them, and re-layouts  147 us (15%)
  waiting for transfers between devices  91.7 us (9%)
  other arithmetic  29.5 us (3%)
  matrix products  29.3 us (3%)
  starting transfers between devices  14.4 us (1%)
    psum x4, blocking collectives, global_sum(): return lax.psum(value, ('gx', 'gy', 'gz'))  316 us
    psum x2, blocking collectives, operate(): root_total = lax.psum(charges, ('gx', 'gy'))  266 us
    psum x1, blocking collectives, body(): lax.psum((jnp.sum(image_two * basis_one), jnp.sum(image_two * basis_two))...  88.2 us
    gather x16, local copies, waits for them, and re-layouts, operate(): ghost_boxes[box_slot[link_index], :, jnp.minimum(body_slot[link_index], g...  68.7 us
    ppermute x4, waiting for transfers between devices, padded(): after = lax.ppermute(leading, axis, down)  52.1 us
    ppermute x4, waiting for transfers between devices, padded(): before = lax.ppermute(last, axis, up)  36.6 us
    gather x16, local copies, waits for them, and re-layouts, operate(): own_value = own_rows[body_slot[link_index]]  29.8 us
    reshape x4, local copies, waits for them, and re-layouts, operate(): ghost_boxes = ghosts.reshape(9, dof_count, ghost_width)  23.4 us
  transfers between devices with their start and end apart: 12, of which 5 were waited for; matrix products, arithmetic and copies ran while one was open for 7% of the time, Pallas kernels for 0%

commit v1 on v0

v1 whole, which is shorter than its diff:
```python
import jax
import jax.numpy as jnp
from jax import lax
from jax.experimental import pallas as pl
from jax.experimental.pallas import tpu as pltpu
from jax.sharding import PartitionSpec as P

F32 = jnp.float32
BF16 = jnp.bfloat16
MESH = pl.DeviceIdType.MESH
epsilon = 1e-06

BLOBS = 162
PITCH = 168
ROWS = 512
BODIES = 256
SKEL = 192
CELLS = 256
RIM = 64
NEIGH = 8
NN = (((1,), (0,)), ((), ()))
NT = (((1,), (1,)), ((), ()))
OFFSETS = [(-1, -1), (-1, 0), (-1, 1), (0, -1), (0, 1), (1, -1), (1, 0), (1, 1)]
PLACE = {offset: index for index, offset in enumerate(OFFSETS)}


def split(x):
    high = x.astype(BF16)
    return high, (x - high.astype(F32)).astype(BF16)


def mm(a, b, dims=NN):
    return lax.dot_general(a, b, dims, preferred_element_type=F32)


def mm3(a, b, dims=NN):
    return mm(a[0], b[0], dims) + (mm(a[0], b[1], dims) + mm(a[1], b[0], dims))


def stacked(x):
    high = x.astype(BF16).astype(F32)
    return jnp.concatenate([high, x - high], axis=0).astype(BF16)


def fold(x):
    half = x.shape[0] // 2
    return x[:half] + x[half:]


def mm_few(x, weights, dims=NN):
    both = stacked(x)
    return fold(mm(both, weights[0], dims) + mm(both, weights[1], dims))


def total(x):
    return jnp.sum(x, axis=(0, 1), keepdims=True)


def iota(shape, dim):
    return lax.broadcasted_iota(jnp.int32, shape, dim)


def frame(angles):
    cos_all, sin_all = jnp.cos(angles), jnp.sin(angles)
    cy, cp, cr = cos_all[0:1], cos_all[1:2], cos_all[2:3]
    sy, sp, sr = sin_all[0:1], sin_all[1:2], sin_all[2:3]
    return (
        (cy * cp, cy * sp * sr - sy * cr, cy * sp * cr + sy * sr),
        (sy * cp, sy * sp * sr + cy * cr, sy * sp * cr - cy * sr),
        (-sp, cp * sr, cp * cr),
    )


def least_squares(beta, diag_first, below_first, above_second, diag_second, below_second):
    first_norm = jnp.sqrt(diag_first * diag_first + below_first * below_first)
    first_cos = diag_first / first_norm
    first_sin = below_first / first_norm
    top_right = first_cos * above_second + first_sin * diag_second
    lower_right = first_cos * diag_second - first_sin * above_second
    second_norm = jnp.sqrt(lower_right * lower_right + below_second * below_second)
    second_cos = lower_right / second_norm
    second_sin = below_second / second_norm
    carried = -first_sin * beta
    coef_two = second_cos * carried / second_norm
    coef_one = (first_cos * beta - top_right * coef_two) / first_norm
    return (coef_one, coef_two, jnp.abs(second_sin * carried))


def kernel(
    sizes,
    rhs_hbm, angles_hbm, self_hbm, near_hbm, weight_hbm, links_hbm, cells_hbm, blob_hbm, perm_hbm, interp_hbm, sibling_hbm, root_hbm,
    u_hbm, coef_ref,
    rhs_in, angles_in, self_in, near_in, weight_in, links_in, cells_in, blob_in, perm_in, interp_in, sibling_in, root_in,
    state_r, state_u, state_t, padded_mat, self_op, near_op, link_op, link_cols, link_rows, occupancy, blob_row, blob_col, rotation,
    perm_row, square, up_op, sibling_op, root_op, own_gather, u_out,
    rim, halo, stage_x, stage_y, stage_z,
    in_sem, out_sem, rim_send, rim_recv, x_send, x_recv, y_send, y_recv, z_send, z_recv,
):
    nx, ny, nz = sizes
    ix, iy, iz = lax.axis_index("gx"), lax.axis_index("gy"), lax.axis_index("gz")
    pending = []

    hbm = [rhs_hbm, blob_hbm, cells_hbm, angles_hbm, self_hbm, near_hbm, weight_hbm, links_hbm, perm_hbm, interp_hbm, sibling_hbm, root_hbm]
    local = [rhs_in, blob_in, cells_in, angles_in, self_in, near_in, weight_in, links_in, perm_in, interp_in, sibling_in, root_in]
    loads = [pltpu.make_async_copy(a, b, in_sem.at[i]) for i, (a, b) in enumerate(zip(hbm, local))]
    for load in loads:
        load.start()
    rhs_load, blob_load, cells_load, angles_load, self_load, near_load = loads[:6]

    def wrapped(index, shift, size):
        return lax.rem(index + shift + size, size)

    barrier = pltpu.get_barrier_semaphore()
    for shift in range(1, nx):
        pl.semaphore_signal(barrier, inc=1, device_id={"gx": wrapped(ix, shift, nx)}, device_id_type=MESH)
    for shift in range(1, ny):
        pl.semaphore_signal(barrier, inc=1, device_id={"gy": wrapped(iy, shift, ny)}, device_id_type=MESH)
    for shift in range(1, nz):
        pl.semaphore_signal(barrier, inc=1, device_id={"gz": iz ^ shift}, device_id_type=MESH)

    state_r[...] = jnp.zeros_like(state_r)
    rhs_load.wait()
    for c in range(3):
        state_r[c * PITCH : c * PITCH + BLOBS, :] = rhs_in[c]
    pl.semaphore_wait(barrier, nx + ny + nz - 3)

    def send(src, dst, send_sem, recv_sem, device):
        copy = pltpu.make_async_remote_copy(
            src_ref=src, dst_ref=dst, send_sem=send_sem, recv_sem=recv_sem, device_id=device, device_id_type=MESH
        )
        copy.start()
        pending.append(copy)
        return copy

    def send_box(phase, source, offset, device, copies):
        place = PLACE[offset]
        copies[offset] = send(
            source, halo.at[phase, place], rim_send.at[phase, place], rim_recv.at[phase, place], device
        )

    def start_halo(phase, state):
        rim[phase] = state[:, :128].T[:RIM]
        copies = {}
        own = rim.at[phase]
        send_box(phase, own, (0, -1), {"gy": wrapped(iy, 1, ny)}, copies)
        send_box(phase, own, (0, 1), {"gy": wrapped(iy, -1, ny)}, copies)
        send_box(phase, own, (-1, 0), {"gx": wrapped(ix, 1, nx)}, copies)
        send_box(phase, own, (1, 0), {"gx": wrapped(ix, -1, nx)}, copies)
        return copies

    def forward_halo(phase, copies, dy):
        copies[(0, dy)].wait_recv()
        box = halo.at[phase, PLACE[(0, dy)]]
        send_box(phase, box, (-1, dy), {"gx": wrapped(ix, 1, nx)}, copies)
        send_box(phase, box, (1, dy), {"gx": wrapped(ix, -1, nx)}, copies)

    def start_x(turn, value):
        stage_x[turn, 0] = value
        return [
            send(stage_x.at[turn, 0], stage_x.at[turn, d], x_send.at[turn, d], x_recv.at[turn, d], {"gx": wrapped(ix, d, nx)})
            for d in range(1, nx)
        ]

    def start_y(turn, value):
        stage_y[turn, 0] = value
        return [
            send(stage_y.at[turn, 0], stage_y.at[turn, d], y_send.at[turn, d], y_recv.at[turn, d], {"gy": wrapped(iy, d, ny)})
            for d in range(1, ny)
        ]

    def start_z(turn, value):
        stage_z[turn, 0] = value
        return [
            send(stage_z.at[turn, 0], stage_z.at[turn, d], z_send.at[turn, d], z_recv.at[turn, d], {"gz": iz ^ d})
            for d in range(1, nz)
        ]

    def summed(copies, stage, turn):
        for copy in copies:
            copy.wait_recv()
        return jnp.sum(stage[turn], axis=0)

    def charges(state):
        rows = [
            jnp.sum(blob_col[...] * state[c * PITCH : (c + 1) * PITCH, :], axis=0, keepdims=True) for c in range(3)
        ]
        moments = jnp.concatenate(rows + [jnp.zeros((5, BODIES), F32)], axis=0)
        return fold(mm(stacked(moments), occupancy[...], NT))

    def far_values(turn, copies):
        for copy in copies:
            copy.wait_recv()
        low_bit = lax.rem(iz, 2) == 1
        high_bit = iz // 2 == 1
        own, one, two, three = (stage_z[turn, d] for d in range(4))
        pick = lambda flag, a, b: jnp.where(flag, a, b)
        joined = jnp.concatenate(
            [
                jnp.concatenate([pick(low_bit, one, own), pick(low_bit, own, one)], axis=1),
                jnp.concatenate([pick(low_bit, three, two), pick(low_bit, two, three)], axis=1),
            ],
            axis=0,
        )
        up = [(up_op[0, level], up_op[1, level]) for level in range(2)]
        siblings = [(sibling_op[0, level], sibling_op[1, level]) for level in range(2)]
        first = mm_few(joined, up[0])
        mine, partner = first[:8], first[8:]
        second = jnp.concatenate([pick(high_bit, partner, mine), pick(high_bit, mine, partner)], axis=1)
        others = mm_few(second, up[1])
        potential = mm_few(others, (root_op[0], root_op[1]))
        placed = mm_few(potential, up[1], NT)
        potential = pick(high_bit, placed[:, CELLS:], placed[:, :CELLS])
        potential = potential + pltpu.roll(mm_few(partner, siblings[1]), 5, axis=0)
        placed = mm_few(potential, up[0], NT)
        potential = pick(low_bit, placed[:, CELLS:], placed[:, :CELLS])
        potential = potential + pltpu.roll(mm_few(one, siblings[0]), 5, axis=0)
        return fold(mm(stacked(potential), occupancy[...]))

    def factor(target, source, inverse):
        index = 3 * source + target if inverse else 3 * target + source
        return rotation[index : index + 1, :]

    def rotated(parts, inverse):
        return [
            factor(target, 0, inverse) * parts[0] + factor(target, 1, inverse) * parts[1] + factor(target, 2, inverse) * parts[2]
            for target in range(3)
        ]

    def write_self(state, result):
        parts = [state[c * PITCH : (c + 1) * PITCH, :] for c in range(3)]
        turned = jnp.concatenate(rotated(parts, False) + [jnp.zeros((ROWS - 3 * PITCH, BODIES), F32)], axis=0)
        mixture = mm3((self_op[0], self_op[1]), split(turned))
        back = rotated([mixture[c * PITCH : (c + 1) * PITCH] for c in range(3)], True)
        for c in range(3):
            result[c * PITCH : (c + 1) * PITCH, :] = back[c]
        result[3 * PITCH :, :] = jnp.zeros((ROWS - 3 * PITCH, BODIES), F32)

    def write_own_gather(state):
        own_gather[...] = mm3((link_op[0, :, :BODIES], link_op[1, :, :BODIES]), split(state[...]), NT)

    def finish(phase, result, values):
        boxes = split(halo[phase].reshape(NEIGH * RIM, ROWS))
        gathered = own_gather[...] + mm3((link_op[0, :, BODIES:], link_op[1, :, BODIES:]), boxes)
        result[...] += mm3((near_op[0], near_op[1]), split(gathered), NT)
        for c in range(3):
            result[c * PITCH : (c + 1) * PITCH, :] += blob_col[...] * values[c : c + 1, :]

    def write_operator(source, target):
        padded_mat[...] = jnp.zeros_like(padded_mat)
        for c in range(3):
            padded_mat[c * PITCH : c * PITCH + BLOBS, : 3 * BLOBS] = source[c * BLOBS : (c + 1) * BLOBS, :]
        matrix = padded_mat[...]
        lane = iota((ROWS, ROWS), 1)
        gap = PITCH - BLOBS
        spread = jnp.where(
            lane < PITCH, matrix, jnp.where(lane < 2 * PITCH, pltpu.roll(matrix, gap, axis=1), pltpu.roll(matrix, 2 * gap, axis=1))
        )
        target[0], target[1] = split(spread)

    def write_square(source, put):
        square[...] = jnp.zeros_like(square)
        square[:SKEL, :SKEL] = source
        put(square[...])

    halo_copies = start_halo(0, state_r)

    blob_load.wait()
    cells_load.wait()
    blob_row[...] = jnp.zeros_like(blob_row)
    blob_row[0:1, :BLOBS] = blob_in[...]
    diagonal = iota((PITCH, BODIES), 0) == iota((PITCH, BODIES), 1)
    column = jnp.sum(jnp.where(diagonal, blob_row[0:1, :], 0.0), axis=1, keepdims=True)
    blob_col[...] = jnp.broadcast_to(column, (PITCH, BODIES))
    occupancy[...] = jnp.where(iota((CELLS, BODIES), 0) == cells_in[...], 1.0, 0.0).astype(BF16)
    own_charges = charges(state_r)
    copies = start_x(0, own_charges)

    angles_load.wait()
    for target, row in enumerate(frame(angles_in[...])):
        for source, value in enumerate(row):
            rotation[3 * target + source : 3 * target + source + 1, :] = value
    self_load.wait()
    write_operator(self_in, self_op)

    copies = start_y(0, summed(copies, stage_x, 0))
    forward_halo(0, halo_copies, 1)

    for load in loads[8:]:
        load.wait()
    lane_few = iota((8, 512), 1)
    perm_row[...] = jnp.full_like(perm_row, -1.0)
    for level in range(2):
        perm = perm_in[level : level + 1, :].astype(F32)
        perm_row[level : level + 1, : 2 * SKEL] = jnp.where(perm >= SKEL, perm + (CELLS - SKEL), perm)
    perm_all = perm_row[...]
    kept_rows = jnp.where(lane_few < SKEL, perm_all, -1.0)[:, :CELLS]
    rest_rows = jnp.where(lane_few < SKEL, pltpu.roll(perm_all, 512 - SKEL, axis=1), -1.0)[:, :CELLS]
    for level in range(2):
        place = iota((2 * CELLS, CELLS), 0).astype(F32)
        kept = jnp.where(place == kept_rows[level : level + 1], 1.0, 0.0)
        rest = jnp.where(place == rest_rows[level : level + 1], 1.0, 0.0).astype(BF16)
        square[...] = jnp.zeros_like(square)
        square[:SKEL, :SKEL] = interp_in[level]
        high, low = split(square[...])
        up_op[0, level], up_op[1, level] = split(kept + (mm(rest, high) + mm(rest, low)))
        square[:SKEL, :SKEL] = sibling_in[level]
        sibling_op[0, level], sibling_op[1, level] = split(square[...])
    square[:SKEL, :SKEL] = root_in[...]
    root_op[0], root_op[1] = split(square[...])

    def start_far_z(turn, column_sum, own):
        return start_z(turn, (column_sum - own) + pltpu.roll(own, 3, axis=0))

    copies = start_far_z(0, summed(copies, stage_y, 0), own_charges)
    forward_halo(0, halo_copies, -1)

    near_load.wait()
    write_operator(near_in, near_op)
    loads[6].wait()
    loads[7].wait()
    links = links_in[...]
    box, body = links // BODIES, lax.rem(links, BODIES)
    place = jnp.where(box < 4, box, box - 1)
    lane_of = jnp.where(box == 4, body, BODIES + place * RIM + body)
    link_rows[...] = jnp.zeros_like(link_rows)
    link_rows[0:NEIGH, :] = lane_of.astype(F32)
    link_rows[NEIGH : 2 * NEIGH, :] = weight_in[...]
    link_cols[...] = link_rows[...].T
    block = 32

    @pl.loop(0, BODIES // block)
    def _(i):
        rows = pl.ds(pl.multiple_of(i * block, block), block)
        entries = link_cols[rows, :]
        width = BODIES + NEIGH * RIM
        lane = iota((block, width), 1).astype(F32)
        weights = jnp.zeros((block, width), F32)
        for k in range(NEIGH):
            weights = weights + jnp.where(lane == entries[:, k : k + 1], entries[:, NEIGH + k : NEIGH + k + 1], 0.0)
        link_op[0, rows, :], link_op[1, rows, :] = split(weights)

    write_self(state_r, state_u)
    write_own_gather(state_r)
    values = far_values(0, copies)
    for copy in halo_copies.values():
        if copy is not halo_copies[(0, 1)] and copy is not halo_copies[(0, -1)]:
            copy.wait_recv()
    finish(0, state_u, values)

    halo_copies = start_halo(1, state_u)
    own_charges = charges(state_u)
    copies = start_x(1, own_charges)
    for c in range(3):
        u_out[c] = state_u[c * PITCH : c * PITCH + BLOBS, :]
    store = pltpu.make_async_copy(u_out, u_hbm, out_sem)
    store.start()
    write_self(state_u, state_t)
    copies = start_y(1, summed(copies, stage_x, 1))
    write_own_gather(state_u)
    forward_halo(1, halo_copies, 1)

    tiny = 1e-30
    rr = total(state_r[...] * state_r[...])
    ru = total(state_r[...] * state_u[...])
    over_rr = jnp.where(rr > 0.0, 1.0 / jnp.where(rr > 0.0, rr, 1.0), 0.0)
    state_u[...] = state_u[...] - (ru * over_rr) * state_r[...]
    uu = total(state_u[...] * state_u[...])
    over_uu = jnp.where(uu > 0.0, 1.0 / jnp.where(uu > 0.0, uu, 1.0), 0.0)

    copies = start_far_z(1, summed(copies, stage_y, 1), own_charges)
    forward_halo(1, halo_copies, -1)
    values = far_values(1, copies)
    for copy in halo_copies.values():
        if copy is not halo_copies[(0, 1)] and copy is not halo_copies[(0, -1)]:
            copy.wait_recv()
    finish(1, state_t, values)

    largest = jnp.maximum(jnp.max(jnp.abs(state_t[...]), axis=(0, 1), keepdims=True), tiny)
    scaled = state_t[...] * (1.0 / largest)
    state_t[...] = scaled
    rt = total(state_r[...] * scaled)
    ut = total(state_u[...] * scaled)
    state_t[...] = state_t[...] - (rt * over_rr) * state_r[...] - (ut * over_uu) * state_u[...]
    tt = total(state_t[...] * state_t[...])
    root_rr, root_uu = jnp.sqrt(rr), jnp.sqrt(uu)
    triangle = [
        root_rr,
        ru * over_rr * root_rr,
        root_uu,
        largest * (rt * over_rr * root_rr),
        largest * (ut * over_uu * root_uu),
        largest * jnp.sqrt(tt),
    ]
    row_of = iota((8, 256), 0)
    lane_is_mine = iota((8, 256), 1) == ix + nx * (iy + ny * iz)
    tile = jnp.zeros((8, 256), F32)
    for i, value in enumerate(triangle):
        tile = jnp.where((row_of == i) & lane_is_mine, value, tile)
    copies = start_x(2, tile)
    copies = start_y(2, summed(copies, stage_x, 2))
    copies = start_z(2, summed(copies, stage_y, 2))
    everyone = summed(copies, stage_z, 2)

    r1, u1, u2, t1, t2, t3 = (everyone[i : i + 1] for i in range(6))
    dot = lambda *pairs: total(sum(a * b for a, b in pairs))
    beta = jnp.sqrt(dot((r1, r1)) + epsilon)
    v1 = r1 / beta
    image1, image2 = v1 + u1 / beta, u2 / beta
    diag_first = dot((image1, v1))
    w1, w2 = image1 - diag_first * v1, image2
    below_first = jnp.sqrt(dot((w1, w1), (w2, w2)) + epsilon)
    second1, second2 = w1 / below_first, w2 / below_first
    rest = (1.0 - diag_first) / beta
    z1 = second1 + (t1 / beta + rest * u1) / below_first
    z2 = second2 + (t2 / beta + rest * u2) / below_first
    z3 = (t3 / beta) / below_first
    above_second = dot((z1, v1))
    diag_second = dot((z1, second1), (z2, second2))
    left1 = z1 - above_second * v1 - diag_second * second1
    left2 = z2 - diag_second * second2
    below_second = jnp.sqrt(dot((left1, left1), (left2, left2), (z3, z3)) + epsilon)
    coef_one, coef_two, residual = least_squares(beta, diag_first, below_first, above_second, diag_second, below_second)
    on_r = coef_one / beta + coef_two * rest / below_first
    on_u = coef_two / (below_first * beta)
    row_few = iota((8, 128), 0)
    coef_ref[...] = jnp.where(row_few == 0, on_r, jnp.where(row_few == 1, on_u, residual))

    store.wait()
    for copy in pending:
        copy.wait_send()


def body(rhs, angles, self_mob, near_mat, near_weight, neighbours, cells, blob_weight, skel_perm, interp, sibling_ops, root_op):
    sizes = tuple(lax.axis_size(axis) for axis in ("gx", "gy", "gz"))
    nx, ny, nz = sizes
    initial = rhs.reshape(3, BLOBS, BODIES)
    operands = [
        initial,
        angles.reshape(3, BODIES),
        self_mob,
        near_mat,
        near_weight.reshape(NEIGH, BODIES),
        neighbours.reshape(NEIGH, BODIES),
        cells.reshape(1, BODIES),
        blob_weight.reshape(1, BLOBS),
        skel_perm,
        interp,
        sibling_ops,
        root_op,
    ]
    vmem = pltpu.VMEM
    dma = pltpu.SemaphoreType.DMA
    u, coefs = pl.pallas_call(
        lambda *refs: kernel(sizes, *refs),
        out_shape=(jax.ShapeDtypeStruct((3, BLOBS, BODIES), F32), jax.ShapeDtypeStruct((8, 128), F32)),
        in_specs=[pl.BlockSpec(memory_space=pl.ANY)] * len(operands),
        out_specs=(pl.BlockSpec(memory_space=pl.ANY), pl.BlockSpec(memory_space=pltpu.VMEM)),
        scratch_shapes=[vmem(x.shape, x.dtype) for x in operands]
        + [
            vmem((ROWS, BODIES), F32),
            vmem((ROWS, BODIES), F32),
            vmem((ROWS, BODIES), F32),
            vmem((ROWS, ROWS), F32),
            vmem((2, ROWS, ROWS), BF16),
            vmem((2, ROWS, ROWS), BF16),
            vmem((2, BODIES, BODIES + NEIGH * RIM), BF16),
            vmem((BODIES, 128), F32),
            vmem((128, BODIES), F32),
            vmem((CELLS, BODIES), BF16),
            vmem((8, BODIES), F32),
            vmem((PITCH, BODIES), F32),
            vmem((16, BODIES), F32),
            vmem((8, 512), F32),
            vmem((CELLS, CELLS), F32),
            vmem((2, 2, 2 * CELLS, CELLS), BF16),
            vmem((2, 2, CELLS, CELLS), BF16),
            vmem((2, CELLS, CELLS), BF16),
            vmem((BODIES, ROWS), F32),
            vmem((3, BLOBS, BODIES), F32),
            vmem((2, RIM, ROWS), F32),
            vmem((2, NEIGH, RIM, ROWS), F32),
            vmem((3, nx, 8, 256), F32),
            vmem((3, ny, 8, 256), F32),
            vmem((3, nz, 8, 256), F32),
            dma((len(operands),)),
            dma(()),
            dma((2, NEIGH)),
            dma((2, NEIGH)),
            dma((3, nx)),
            dma((3, nx)),
            dma((3, ny)),
            dma((3, ny)),
            dma((3, nz)),
            dma((3, nz)),
        ],
        compiler_params=pltpu.CompilerParams(collective_id=0, has_side_effects=True, vmem_limit_bytes=48 * 2**20),
    )(*operands)
    result = coefs[0, 0] * initial + coefs[1, 0] * u
    return (result[None, None], coefs[2, 0])


def solution(mesh):
    in_specs = (
        P("gx", "gy", None, None, "gz"),
        P("gx", "gy", None, "gz"),
        P(),
        P(),
        P("gx", "gy", None, "gz"),
        P("gx", "gy", None, "gz"),
        P("gx", "gy", "gz"),
        P(),
        P(),
        P(),
        P(),
        P(),
    )
    out_specs = (P("gx", "gy", None, None, "gz"), P())
    return jax.shard_map(body, mesh=mesh, in_specs=in_specs, out_specs=out_specs, check_vma=False)
```

time: 1000 us -> 69.2 us (0.07)
  blocking collectives: 671 us -> 0 us
  local copies, waits for them, and re-layouts: 147 us -> 8.5 us
  waiting for transfers between devices: 91.7 us -> 0 us
  Pallas kernels: 0 us -> 58.3 us
  matrix products: 29.3 us -> 0 us
  other arithmetic: 29.5 us -> 1.38 us
  starting transfers between devices: 14.4 us -> 0 us
    psum x7 -> x0, blocking collectives: 671 us -> none  [the longest x4 316 us: global_sum(): return lax.psum(value, ('gx', 'gy', 'gz'))]
    gather x32 -> x0, local copies, waits for them, and re-layouts: 98.5 us -> none  [the longest x16 68.7 us: operate(): ghost_boxes[box_slot[link_index], :, jnp.minimum(body_slot[link_index], g...]
    ppermute x12 -> x0, waiting for transfers between devices: 91.7 us -> none  [the longest x4 52.1 us: padded(): after = lax.ppermute(leading, axis, down)]
    pallas_call x0 -> x1, Pallas kernels: none -> 58.3 us  [body(): pl.pallas_call(lambda *refs: kernel(sizes, *refs), out_shape=(jax.ShapeDt...]
    dot_general x32 -> x0, matrix products: 29.3 us -> none  [the longest x12 17.3 us: contract_last(): lax.dot_general(left, right, (((1,), (1,)), ((), ())), precision=highest)]
    reshape x8 -> x0, local copies, waits for them, and re-layouts: 26.7 us -> none  [the longest x4 23.4 us: operate(): ghost_boxes = ghosts.reshape(9, dof_count, ghost_width)]
    ppermute x12 -> x0, starting transfers between devices: 14.4 us -> none  [the longest x4 8.22 us: padded(): after = lax.ppermute(leading, axis, down)]
    concatenate x5 -> x0, other arithmetic: 10.3 us -> none  [the longest x4 10.2 us: padded(): shard = jnp.concatenate([before, shard, after], axis=dim)]
  transfers between devices with their start and end apart: 12 -> 0, of which waited for: 5 -> 0; matrix products, arithmetic and copies ran while one was open for 7% -> 0% of each run, Pallas kernels for 0% -> 0%
where the time goes in v1:
time: 69.2 us; the launch traced here: 68.9 us
  Pallas kernels  58.3 us (84%)
  local copies, waits for them, and re-layouts  8.5 us (12%)
  other arithmetic  1.38 us (2%)
  between operations  0.71 us (1%)
    pallas_call x1, Pallas kernels, body(): pl.pallas_call(lambda *refs: kernel(sizes, *refs), out_shape=(jax.ShapeDt...  58.3 us
    unnamed x25, local copies, waits for them, and re-layouts  7.95 us

profile of v1, /device:TPU:1, one launch (start us, length us, event | category | flops | bytes accessed | tf_op | source)
XLA Modules:
  0.0 68.9 jit_solution(4221617153707462490)
XLA Ops:
  0.6 0.0 copy-start
  0.6 0.8 %copy.22 = f32[1,1,3,256]{3,2,1,0:T(4,128)S(1)} copy(f32[1,1,3,256]{3,1,2,0:T(1,128)} %param.13) | data formatting | bytes 6144
  1.4 0.0 copy-start.5
  1.4 0.0 copy-start.6
  1.4 0.0 copy-start.7
  1.4 0.0 copy-start.9
  1.4 1.1 %copy.21 = f32[1,1,3,162,256]{4,3,1,2,0:T(8,128)S(1)} copy(f32[1,1,3,162,256]{4,1,3,2,0:T(1,128)} %param.12) | data formatting | bytes 995328
  2.5 0.0 copy-start.8
  2.6 0.0 copy-done
  2.6 0.0 copy-done.5
  2.6 0.0 copy-done.6
  2.6 0.0 copy-done.7
  2.6 0.0 copy-done.9
  2.6 0.6 copy-done.8
  3.2 0.0 copy-start.1
  3.2 1.2 %copy-done.1 = f32[486,486]{1,0:T(8,128)S(1)} copy-done((f32[486,486]{1,0:T(8,128)S(1)}, f32[486,486]{1,0:T(8,128)}, u32[]{:S(2)}) %copy-start.1) | copy-done | bytes 944808
  4.4 0.0 copy-start.2
  4.4 1.0 %copy-done.2 = f32[2,192,192]{2,1,0:T(8,128)S(1)} copy-done((f32[2,192,192]{2,1,0:T(8,128)S(1)}, f32[2,192,192]{2,1,0:T(8,128)}, u32[]{:S(2)}) %copy-start.2) | copy-done | bytes 294936
  5.4 0.0 copy-start.3
  5.4 1.0 %copy-done.3 = f32[2,192,192]{2,1,0:T(8,128)S(1)} copy-done((f32[2,192,192]{2,1,0:T(8,128)S(1)}, f32[2,192,192]{2,1,0:T(8,128)}, u32[]{:S(2)}) %copy-start.3) | copy-done | bytes 294936
  6.4 0.0 copy-start.4
  6.4 0.9 %copy-done.4 = f32[192,192]{1,0:T(8,128)S(1)} copy-done((f32[192,192]{1,0:T(8,128)S(1)}, f32[192,192]{1,0:T(8,128)}, u32[]{:S(2)}) %copy-start.4) | copy-done | bytes 147480
  7.4 0.0 copy-start.10
  7.4 58.3 %shard_map.131 = (f32[3,162,256]{2,1,0:T(8,128)S(1)}, f32[8,128]{1,0:T(8,128)S(1)}) custom-call(f32[3,162,256]{2,1,0:T(8,128)S(1)} %bitcast.17, f32[3,256]{1,0:T(4,128)S(1)} %bitcast.18, f32[486,486]{1,0:T(8,128)S(1)} %copy-done, f32[486,486]{1,0:T(8,128)S(1)} %copy-done.1, f32[8,256]{1,0:T(8,128)S(1)} %bitcast.19, s32[8,256]{1,0:T(8,128)S(1)} %bitcast.20, ...), custom_call_target="tpu_custom_call" | custom-call | tf_op jit(solution)/shard_map/pallas_call | solution.py:453
  65.6 0.5 fusion
  66.2 0.0 copy-done.10
  66.2 1.4 %add_bitcast_fusion = f32[1,1,3,162,256]{4,3,2,1,0:T(8,128)S(1)} fusion(f32[3,162,256]{2,1,0:T(8,128)S(1)} %get-tuple-element.5, f32[]{:T(128)} %bitcast.5, f32[]{:T(128)} %bitcast.4, f32[1,1,3,162,256]{4,1,3,2,0:T(1,128)S(1)} %copy-done.10), kind=kLoop, calls=%fused_computation.1 | loop fusion | flops 373248 | bytes 1493000 | tf_op jit(solution)/shard_map/broadcast_in_dim | solution.py:499
  67.6 1.3 %copy.14 = f32[1,1,3,162,256]{4,1,3,2,0:T(1,128)} copy(f32[1,1,3,162,256]{4,3,2,1,0:T(8,128)S(1)} %add_bitcast_fusion) | data formatting | bytes 995328
Async XLA Ops:
  0.6 1.9 %copy-start = (f32[486,486]{1,0:T(8,128)S(1)}, f32[486,486]{1,0:T(8,128)}, u32[]{:S(2)}) copy-start(f32[486,486]{1,0:T(8,128)} %refs_2_.1) | copy-start | bytes 2834356
  1.4 1.2 %copy-start.5 = (f32[1,1,8,256]{3,2,1,0:T(8,128)S(1)}, f32[1,1,8,256]{3,2,1,0:T(8,128)}, u32[]{:S(2)}) copy-start(f32[1,1,8,256]{3,2,1,0:T(8,128)} %param.16) | copy-start | bytes 24580
  1.4 1.2 %copy-start.6 = (s32[1,1,8,256]{3,2,1,0:T(8,128)S(1)}, s32[1,1,8,256]{3,2,1,0:T(8,128)}, u32[]{:S(2)}) copy-start(s32[1,1,8,256]{3,2,1,0:T(8,128)} %param.17) | copy-start | bytes 24580
  1.4 1.2 %copy-start.7 = (s32[2,384]{1,0:T(2,128)S(1)}, s32[2,384]{1,0:T(2,128)}, u32[]{:S(2)}) copy-start(s32[2,384]{1,0:T(2,128)} %refs_8_.1) | copy-start | bytes 9220
  1.4 1.2 %copy-start.9 = (f32[162]{0:T(256)S(1)}, f32[162]{0:T(256)}, u32[]{:S(2)}) copy-start(f32[162]{0:T(256)} %param.19) | copy-start | bytes 1948
  2.5 0.7 copy-start.8
  3.2 1.2 %copy-start.1 = (f32[486,486]{1,0:T(8,128)S(1)}, f32[486,486]{1,0:T(8,128)}, u32[]{:S(2)}) copy-start(f32[486,486]{1,0:T(8,128)} %refs_3_.1) | copy-start | bytes 2834356
  4.4 1.0 %copy-start.2 = (f32[2,192,192]{2,1,0:T(8,128)S(1)}, f32[2,192,192]{2,1,0:T(8,128)}, u32[]{:S(2)}) copy-start(f32[2,192,192]{2,1,0:T(8,128)} %refs_9_.1) | copy-start | bytes 884740
  5.4 1.0 %copy-start.3 = (f32[2,192,192]{2,1,0:T(8,128)S(1)}, f32[2,192,192]{2,1,0:T(8,128)}, u32[]{:S(2)}) copy-start(f32[2,192,192]{2,1,0:T(8,128)} %refs_10_.1) | copy-start | bytes 884740
  6.4 0.9 %copy-start.4 = (f32[192,192]{1,0:T(8,128)S(1)}, f32[192,192]{1,0:T(8,128)}, u32[]{:S(2)}) copy-start(f32[192,192]{1,0:T(8,128)} %refs_11_.1) | copy-start | bytes 442372
  7.4 58.8 %copy-start.10 = (f32[1,1,3,162,256]{4,1,3,2,0:T(1,128)S(1)}, f32[1,1,3,162,256]{4,1,3,2,0:T(1,128)}, u32[]{:S(2)}) copy-start(f32[1,1,3,162,256]{4,1,3,2,0:T(1,128)} %param.12) | copy-start | bytes 1492996

commit v2 on v1

--- a/solution.py
+++ b/solution.py
@@ -20,8 +20,7 @@
 NEIGH = 8
 NN = (((1,), (0,)), ((), ()))
 NT = (((1,), (1,)), ((), ()))
-OFFSETS = [(-1, -1), (-1, 0), (-1, 1), (0, -1), (0, 1), (1, -1), (1, 0), (1, 1)]
-PLACE = {offset: index for index, offset in enumerate(OFFSETS)}
+PARTS = 2
 
 
 def split(x):
@@ -86,99 +85,146 @@
     return (coef_one, coef_two, jnp.abs(second_sin * carried))
 
 
+CORE = [(0, 1, 0, 0, 0)]
+PLANE = [(y, 0, x, 0, 0) for y in range(4) for x in range(4) if x or y]
+DEPTH = [(0, 0, 0, low, high) for low in range(2) for high in range(4) if low or high]
+
+
+def ring(step, size):
+    return min(step % size, -step % size)
+
+
+def hops(offset):
+    y, _, x, low, high = offset
+    return ring(y, 4) + ring(x, 4) + ring(2 * high + low, 8)
+
+
 def kernel(
-    sizes,
     rhs_hbm, angles_hbm, self_hbm, near_hbm, weight_hbm, links_hbm, cells_hbm, blob_hbm, perm_hbm, interp_hbm, sibling_hbm, root_hbm,
-    u_hbm, coef_ref,
+    u_hbm, on_r_ref, on_u_ref, residual_ref,
     rhs_in, angles_in, self_in, near_in, weight_in, links_in, cells_in, blob_in, perm_in, interp_in, sibling_in, root_in,
-    state_r, state_u, state_t, padded_mat, self_op, near_op, link_op, link_cols, link_rows, occupancy, blob_row, blob_col, rotation,
-    perm_row, square, up_op, sibling_op, root_op, own_gather, u_out,
-    rim, halo, stage_x, stage_y, stage_z,
-    in_sem, out_sem, rim_send, rim_recv, x_send, x_recv, y_send, y_recv, z_send, z_recv,
+    state_r, state_u, state_t, padded_mat, self_op, near_op, link_op, link_cols, link_rows, occupancy, blob_row, blob_rows, blob_col,
+    rotation, perm_row, square, up_op, sibling_op, root_op, own_gather, self_rim, u_out,
+    rim, halo, stage_c, stage_p, stage_d,
+    in_sem, out_sem, rim_send, rim_recv, c_send, c_recv, p_send, p_recv, d_send, d_recv,
 ):
-    nx, ny, nz = sizes
     ix, iy, iz = lax.axis_index("gx"), lax.axis_index("gy"), lax.axis_index("gz")
     pending = []
 
-    hbm = [rhs_hbm, blob_hbm, cells_hbm, angles_hbm, self_hbm, near_hbm, weight_hbm, links_hbm, perm_hbm, interp_hbm, sibling_hbm, root_hbm]
-    local = [rhs_in, blob_in, cells_in, angles_in, self_in, near_in, weight_in, links_in, perm_in, interp_in, sibling_in, root_in]
-    loads = [pltpu.make_async_copy(a, b, in_sem.at[i]) for i, (a, b) in enumerate(zip(hbm, local))]
-    for load in loads:
+    def body_rows(c):
+        return slice(c * PITCH, c * PITCH + BLOBS)
+
+    def pad_rows(c):
+        return slice(c * PITCH + BLOBS, (c + 1) * PITCH if c < 2 else ROWS)
+
+    for c in range(3):
+        state_r[pad_rows(c), :] = jnp.zeros_like(state_r[pad_rows(c), :])
+    pairs = {
+        "rhs": (rhs_hbm.at[:, :, 0, :], rhs_in),
+        "blob": (blob_hbm, blob_in),
+        "cells": (cells_hbm, cells_in),
+        "angles": (angles_hbm.at[:, 0, :], angles_in),
+        "self": (self_hbm, self_in),
+        "weight": (weight_hbm, weight_in),
+        "links": (links_hbm, links_in),
+        "perm": (perm_hbm, perm_in),
+        "interp": (interp_hbm, interp_in),
+        "sibling": (sibling_hbm, sibling_in),
+        "root": (root_hbm, root_in),
+        "near": (near_hbm, near_in),
+    }
+    loads = {name: pltpu.make_async_copy(a, b, in_sem.at[i]) for i, (name, (a, b)) in enumerate(pairs.items())}
+    for load in loads.values():
         load.start()
-    rhs_load, blob_load, cells_load, angles_load, self_load, near_load = loads[:6]
 
     def wrapped(index, shift, size):
         return lax.rem(index + shift + size, size)
 
+    odd = lax.rem(iy, 2)
+    plus, minus = {"gx": wrapped(ix, 1, 8)}, {"gx": wrapped(ix, -1, 8)}
+    across = {"gy": wrapped(iy, 2 * odd - 1, 8)}
+    beside = {"gy": iy + 1 - 2 * odd}
+    far_gx = {"gx": wrapped(ix, 2 * lax.rem(ix, 2) - 1, 8)}
+
+    def peer(offset):
+        y, core, x, low, high = offset
+        device = {}
+        if y or core:
+            device["gx"] = 2 * lax.rem(ix // 2 + y, 4) + lax.rem(ix + core, 2)
+        if x or low:
+            device["gy"] = 2 * lax.rem(iy // 2 + x, 4) + lax.rem(iy + low, 2)
+        if high:
+            device["gz"] = iz ^ high
+        return device
+
     barrier = pltpu.get_barrier_semaphore()
-    for shift in range(1, nx):
-        pl.semaphore_signal(barrier, inc=1, device_id={"gx": wrapped(ix, shift, nx)}, device_id_type=MESH)
-    for shift in range(1, ny):
-        pl.semaphore_signal(barrier, inc=1, device_id={"gy": wrapped(iy, shift, ny)}, device_id_type=MESH)
-    for shift in range(1, nz):
-        pl.semaphore_signal(barrier, inc=1, device_id={"gz": iz ^ shift}, device_id_type=MESH)
-
-    state_r[...] = jnp.zeros_like(state_r)
-    rhs_load.wait()
-    for c in range(3):
-        state_r[c * PITCH : c * PITCH + BLOBS, :] = rhs_in[c]
-    pl.semaphore_wait(barrier, nx + ny + nz - 3)
-
-    def send(src, dst, send_sem, recv_sem, device):
-        copy = pltpu.make_async_remote_copy(
+    greeted = [across, far_gx] + [peer(o) for o in sorted(DEPTH + PLANE + CORE, key=hops, reverse=True)]
+    for device in greeted:
+        pl.semaphore_signal(barrier, inc=1, device_id=device, device_id_type=MESH)
+
+    def remote(src, dst, send_sem, recv_sem, device):
+        return pltpu.make_async_remote_copy(
             src_ref=src, dst_ref=dst, send_sem=send_sem, recv_sem=recv_sem, device_id=device, device_id_type=MESH
         )
+
+    def send(*what):
+        copy = remote(*what)
         copy.start()
         pending.append(copy)
         return copy
 
-    def send_box(phase, source, offset, device, copies):
-        place = PLACE[offset]
-        copies[offset] = send(
-            source, halo.at[phase, place], rim_send.at[phase, place], rim_recv.at[phase, place], device
-        )
-
-    def start_halo(phase, state):
-        rim[phase] = state[:, :128].T[:RIM]
-        copies = {}
+    part = RIM // PARTS
+
+    def box_copy(phase, source, place, i, device):
+        rows = pl.ds(i * part, part)
+        return (source.at[rows], halo.at[phase, place, rows], rim_send.at[phase, place, i], rim_recv.at[phase, place, i], device)
+
+    def start_halo(phase):
         own = rim.at[phase]
-        send_box(phase, own, (0, -1), {"gy": wrapped(iy, 1, ny)}, copies)
-        send_box(phase, own, (0, 1), {"gy": wrapped(iy, -1, ny)}, copies)
-        send_box(phase, own, (-1, 0), {"gx": wrapped(ix, 1, nx)}, copies)
-        send_box(phase, own, (1, 0), {"gx": wrapped(ix, -1, nx)}, copies)
-        return copies
-
-    def forward_halo(phase, copies, dy):
-        copies[(0, dy)].wait_recv()
-        box = halo.at[phase, PLACE[(0, dy)]]
-        send_box(phase, box, (-1, dy), {"gx": wrapped(ix, 1, nx)}, copies)
-        send_box(phase, box, (1, dy), {"gx": wrapped(ix, -1, nx)}, copies)
-
-    def start_x(turn, value):
-        stage_x[turn, 0] = value
-        return [
-            send(stage_x.at[turn, 0], stage_x.at[turn, d], x_send.at[turn, d], x_recv.at[turn, d], {"gx": wrapped(ix, d, nx)})
-            for d in range(1, nx)
+        for i in range(PARTS):
+            send(*box_copy(phase, own, 3 + odd, i, beside))
+        for i in range(PARTS):
+            send(*box_copy(phase, own, 4 - odd, i, across))
+        for i in range(PARTS):
+            send(*box_copy(phase, own, 1, i, plus))
+            send(*box_copy(phase, own, 6, i, minus))
+
+    def forward_halo(phase, place):
+        box = halo.at[phase, place]
+        for i in range(PARTS):
+            remote(*box_copy(phase, rim.at[phase], place, i, plus)).wait_recv()
+            send(*box_copy(phase, box, 2 * (place - 3), i, plus))
+            send(*box_copy(phase, box, 2 * (place - 3) + 5, i, minus))
+
+    def wait_boxes(phase):
+        for place in (1, 6, 0, 5, 2, 7):
+            for i in range(PARTS):
+                remote(*box_copy(phase, rim.at[phase], place, i, plus)).wait_recv()
+
+    def exchange(stage, send_sem, recv_sem, group, turn, value):
+        stage[turn, 0] = value
+        order = sorted(range(len(group)), key=lambda i: -hops(group[i]))
+        copies = [
+            send(stage.at[turn, 0], stage.at[turn, i + 1], send_sem.at[turn, i], recv_sem.at[turn, i], peer(group[i])) for i in order
         ]
-
-    def start_y(turn, value):
-        stage_y[turn, 0] = value
-        return [
-            send(stage_y.at[turn, 0], stage_y.at[turn, d], y_send.at[turn, d], y_recv.at[turn, d], {"gy": wrapped(iy, d, ny)})
-            for d in range(1, ny)
-        ]
-
-    def start_z(turn, value):
-        stage_z[turn, 0] = value
-        return [
-            send(stage_z.at[turn, 0], stage_z.at[turn, d], z_send.at[turn, d], z_recv.at[turn, d], {"gz": iz ^ d})
-            for d in range(1, nz)
-        ]
+        return copies[::-1]
+
+    def start_core(turn, value):
+        return exchange(stage_c, c_send, c_recv, CORE, turn, value)
+
+    def start_plane(turn, value):
+        return exchange(stage_p, p_send, p_recv, PLANE, turn, value)
+
+    def start_depth(turn, value):
+        return exchange(stage_d, d_send, d_recv, DEPTH, turn, value)
 
     def summed(copies, stage, turn):
         for copy in copies:
             copy.wait_recv()
         return jnp.sum(stage[turn], axis=0)
+
+    def start_far(turn, copies, own):
+        return start_depth(turn, summed(copies, stage_p, turn) + pltpu.roll(own, 3, axis=0))
 
     def charges(state):
         rows = [
@@ -192,7 +238,13 @@
             copy.wait_recv()
         low_bit = lax.rem(iz, 2) == 1
         high_bit = iz // 2 == 1
-        own, one, two, three = (stage_z[turn, d] for d in range(4))
+        top = iota((8, CELLS), 0) < 3
+        layers = []
+        for high in range(4):
+            here = stage_d[turn, DEPTH.index((0, 0, 0, 0, high)) + 1 if high else 0]
+            there = stage_d[turn, DEPTH.index((0, 0, 0, 1, high)) + 1]
+            layers.append(jnp.where(top, here + there - pltpu.roll(here, 5, axis=0), here))
+        own, one, two, three = layers
         pick = lambda flag, a, b: jnp.where(flag, a, b)
         joined = jnp.concatenate(
             [
@@ -238,10 +290,17 @@
     def write_own_gather(state):
         own_gather[...] = mm3((link_op[0, :, :BODIES], link_op[1, :, :BODIES]), split(state[...]), NT)
 
-    def finish(phase, result, values):
-        boxes = split(halo[phase].reshape(NEIGH * RIM, ROWS))
-        gathered = own_gather[...] + mm3((link_op[0, :, BODIES:], link_op[1, :, BODIES:]), boxes)
-        result[...] += mm3((near_op[0], near_op[1]), split(gathered), NT)
+    def boxes_of(phase):
+        return split(halo[phase].reshape(NEIGH * RIM, ROWS))
+
+    def gathered(bodies, boxes):
+        return own_gather[:bodies, :] + mm3((link_op[0, :bodies, BODIES:], link_op[1, :bodies, BODIES:]), boxes)
+
+    def near_pair():
+        return (near_op[0], near_op[1])
+
+    def finish(result, boxes, values):
+        result[...] += mm3(near_pair(), split(gathered(BODIES, boxes)), NT)
         for c in range(3):
             result[c * PITCH : (c + 1) * PITCH, :] += blob_col[...] * values[c : c + 1, :]
 
@@ -257,37 +316,38 @@
         )
         target[0], target[1] = split(spread)
 
-    def write_square(source, put):
-        square[...] = jnp.zeros_like(square)
-        square[:SKEL, :SKEL] = source
-        put(square[...])
-
-    halo_copies = start_halo(0, state_r)
-
-    blob_load.wait()
-    cells_load.wait()
+    loads["rhs"].wait()
+    for c in range(3):
+        state_r[body_rows(c), :] = rhs_in[c]
+    rim[0] = state_r[:, :128].T[:RIM]
+    pl.semaphore_wait(barrier, len(greeted))
+    start_halo(0)
+
+    loads["blob"].wait()
+    loads["cells"].wait()
     blob_row[...] = jnp.zeros_like(blob_row)
     blob_row[0:1, :BLOBS] = blob_in[...]
     diagonal = iota((PITCH, BODIES), 0) == iota((PITCH, BODIES), 1)
-    column = jnp.sum(jnp.where(diagonal, blob_row[0:1, :], 0.0), axis=1, keepdims=True)
+    column = jnp.sum(jnp.where(diagonal, blob_row[0:1, :BODIES], 0.0), axis=1, keepdims=True)
     blob_col[...] = jnp.broadcast_to(column, (PITCH, BODIES))
     occupancy[...] = jnp.where(iota((CELLS, BODIES), 0) == cells_in[...], 1.0, 0.0).astype(BF16)
     own_charges = charges(state_r)
-    copies = start_x(0, own_charges)
-
-    angles_load.wait()
+    copies = start_core(0, own_charges)
+
+    loads["angles"].wait()
     for target, row in enumerate(frame(angles_in[...])):
         for source, value in enumerate(row):
             rotation[3 * target + source : 3 * target + source + 1, :] = value
-    self_load.wait()
+    copies = start_plane(0, summed(copies, stage_c, 0))
+    loads["self"].wait()
     write_operator(self_in, self_op)
 
-    copies = start_y(0, summed(copies, stage_x, 0))
-    forward_halo(0, halo_copies, 1)
-
-    for load in loads[8:]:
-        load.wait()
+    for name in ("perm", "interp", "sibling", "root"):
+        loads[name].wait()
     lane_few = iota((8, 512), 1)
+    blob_first = blob_row[...]
+    for c in range(3):
+        blob_rows[c : c + 1, :] = pltpu.roll(blob_first, c * PITCH, axis=1)[0:1] if c else blob_first[0:1]
     perm_row[...] = jnp.full_like(perm_row, -1.0)
     for level in range(2):
         perm = perm_in[level : level + 1, :].astype(F32)
@@ -295,11 +355,11 @@
     perm_all = perm_row[...]
     kept_rows = jnp.where(lane_few < SKEL, perm_all, -1.0)[:, :CELLS]
     rest_rows = jnp.where(lane_few < SKEL, pltpu.roll(perm_all, 512 - SKEL, axis=1), -1.0)[:, :CELLS]
+    square[...] = jnp.zeros_like(square)
     for level in range(2):
         place = iota((2 * CELLS, CELLS), 0).astype(F32)
         kept = jnp.where(place == kept_rows[level : level + 1], 1.0, 0.0)
         rest = jnp.where(place == rest_rows[level : level + 1], 1.0, 0.0).astype(BF16)
-        square[...] = jnp.zeros_like(square)
         square[:SKEL, :SKEL] = interp_in[level]
         high, low = split(square[...])
         up_op[0, level], up_op[1, level] = split(kept + (mm(rest, high) + mm(rest, low)))
@@ -308,16 +368,14 @@
     square[:SKEL, :SKEL] = root_in[...]
     root_op[0], root_op[1] = split(square[...])
 
-    def start_far_z(turn, column_sum, own):
-        return start_z(turn, (column_sum - own) + pltpu.roll(own, 3, axis=0))
-
-    copies = start_far_z(0, summed(copies, stage_y, 0), own_charges)
-    forward_halo(0, halo_copies, -1)
-
-    near_load.wait()
-    write_operator(near_in, near_op)
-    loads[6].wait()
-    loads[7].wait()
+    forward_halo(0, 4 - odd)
+    copies = start_far(0, copies, own_charges)
+    write_self(state_r, state_u)
+    self_rim[...] = state_u[:, :128].T[:RIM]
+    forward_halo(0, 3 + odd)
+
+    loads["weight"].wait()
+    loads["links"].wait()
     links = links_in[...]
     box, body = links // BODIES, lax.rem(links, BODIES)
     place = jnp.where(box < 4, box, box - 1)
@@ -339,41 +397,42 @@
             weights = weights + jnp.where(lane == entries[:, k : k + 1], entries[:, NEIGH + k : NEIGH + k + 1], 0.0)
         link_op[0, rows, :], link_op[1, rows, :] = split(weights)
 
-    write_self(state_r, state_u)
+    loads["near"].wait()
+    write_operator(near_in, near_op)
     write_own_gather(state_r)
     values = far_values(0, copies)
-    for copy in halo_copies.values():
-        if copy is not halo_copies[(0, 1)] and copy is not halo_copies[(0, -1)]:
-            copy.wait_recv()
-    finish(0, state_u, values)
-
-    halo_copies = start_halo(1, state_u)
+    wait_boxes(0)
+
+    boxes = boxes_of(0)
+    columns = jnp.concatenate([values, jnp.zeros((120, BODIES), F32)], axis=0)[:, :128].T[:RIM]
+    far_rim = sum(columns[:, c : c + 1] * blob_rows[c : c + 1, :] for c in range(3))
+    rim[1] = self_rim[...] + mm3(split(gathered(RIM, boxes)), near_pair(), NT) + far_rim
+    start_halo(1)
+    finish(state_u, boxes, values)
     own_charges = charges(state_u)
-    copies = start_x(1, own_charges)
+    copies = start_core(1, own_charges)
     for c in range(3):
-        u_out[c] = state_u[c * PITCH : c * PITCH + BLOBS, :]
-    store = pltpu.make_async_copy(u_out, u_hbm, out_sem)
+        u_out[c] = state_u[body_rows(c), :]
+    store = pltpu.make_async_copy(u_out, u_hbm.at[:, :, 0, :], out_sem)
     store.start()
     write_self(state_u, state_t)
-    copies = start_y(1, summed(copies, stage_x, 1))
+    copies = start_plane(1, summed(copies, stage_c, 1))
+    forward_halo(1, 4 - odd)
     write_own_gather(state_u)
-    forward_halo(1, halo_copies, 1)
 
     tiny = 1e-30
     rr = total(state_r[...] * state_r[...])
     ru = total(state_r[...] * state_u[...])
     over_rr = jnp.where(rr > 0.0, 1.0 / jnp.where(rr > 0.0, rr, 1.0), 0.0)
+    forward_halo(1, 3 + odd)
     state_u[...] = state_u[...] - (ru * over_rr) * state_r[...]
     uu = total(state_u[...] * state_u[...])
     over_uu = jnp.where(uu > 0.0, 1.0 / jnp.where(uu > 0.0, uu, 1.0), 0.0)
 
-    copies = start_far_z(1, summed(copies, stage_y, 1), own_charges)
-    forward_halo(1, halo_copies, -1)
+    copies = start_far(1, copies, own_charges)
     values = far_values(1, copies)
-    for copy in halo_copies.values():
-        if copy is not halo_copies[(0, 1)] and copy is not halo_copies[(0, -1)]:
-            copy.wait_recv()
-    finish(1, state_t, values)
+    wait_boxes(1)
+    finish(state_t, boxes_of(1), values)
 
     largest = jnp.maximum(jnp.max(jnp.abs(state_t[...]), axis=(0, 1), keepdims=True), tiny)
     scaled = state_t[...] * (1.0 / largest)
@@ -392,14 +451,14 @@
         largest * jnp.sqrt(tt),
     ]
     row_of = iota((8, 256), 0)
-    lane_is_mine = iota((8, 256), 1) == ix + nx * (iy + ny * iz)
+    lane_is_mine = iota((8, 256), 1) == ix + 8 * (iy + 8 * iz)
     tile = jnp.zeros((8, 256), F32)
     for i, value in enumerate(triangle):
         tile = jnp.where((row_of == i) & lane_is_mine, value, tile)
-    copies = start_x(2, tile)
-    copies = start_y(2, summed(copies, stage_x, 2))
-    copies = start_z(2, summed(copies, stage_y, 2))
-    everyone = summed(copies, stage_z, 2)
+    copies = start_core(2, tile)
+    copies = start_plane(2, summed(copies, stage_c, 2))
+    copies = start_depth(2, summed(copies, stage_p, 2))
+    everyone = summed(copies, stage_d, 2)
 
     r1, u1, u2, t1, t2, t3 = (everyone[i : i + 1] for i in range(6))
     dot = lambda *pairs: total(sum(a * b for a, b in pairs))
@@ -422,8 +481,9 @@
     coef_one, coef_two, residual = least_squares(beta, diag_first, below_first, above_second, diag_second, below_second)
     on_r = coef_one / beta + coef_two * rest / below_first
     on_u = coef_two / (below_first * beta)
-    row_few = iota((8, 128), 0)
-    coef_ref[...] = jnp.where(row_few == 0, on_r, jnp.where(row_few == 1, on_u, residual))
+    on_r_ref[...] = jnp.broadcast_to(on_r, (1, BODIES))
+    on_u_ref[...] = jnp.broadcast_to(on_u, (1, BODIES))
+    residual_ref[...] = residual
 
     store.wait()
     for copy in pending:
@@ -431,12 +491,10 @@
 
 
 def body(rhs, angles, self_mob, near_mat, near_weight, neighbours, cells, blob_weight, skel_perm, interp, sibling_ops, root_op):
-    sizes = tuple(lax.axis_size(axis) for axis in ("gx", "gy", "gz"))
-    nx, ny, nz = sizes
-    initial = rhs.reshape(3, BLOBS, BODIES)
+    initial = rhs.reshape(3, BLOBS, 1, BODIES)
     operands = [
         initial,
-        angles.reshape(3, BODIES),
+        angles.reshape(3, 1, BODIES),
         self_mob,
         near_mat,
         near_weight.reshape(NEIGH, BODIES),
@@ -450,12 +508,23 @@
     ]
     vmem = pltpu.VMEM
     dma = pltpu.SemaphoreType.DMA
-    u, coefs = pl.pallas_call(
-        lambda *refs: kernel(sizes, *refs),
-        out_shape=(jax.ShapeDtypeStruct((3, BLOBS, BODIES), F32), jax.ShapeDtypeStruct((8, 128), F32)),
-        in_specs=[pl.BlockSpec(memory_space=pl.ANY)] * len(operands),
-        out_specs=(pl.BlockSpec(memory_space=pl.ANY), pl.BlockSpec(memory_space=pltpu.VMEM)),
-        scratch_shapes=[vmem(x.shape, x.dtype) for x in operands]
+    u, on_r, on_u, residual = pl.pallas_call(
+        kernel,
+        out_shape=(
+            jax.ShapeDtypeStruct(initial.shape, F32),
+            jax.ShapeDtypeStruct((1, BODIES), F32),
+            jax.ShapeDtypeStruct((1, BODIES), F32),
+            jax.ShapeDtypeStruct((1, 1), F32),
+        ),
+        in_specs=[pl.BlockSpec(memory_space=pltpu.HBM)] * len(operands),
+        out_specs=(
+            pl.BlockSpec(memory_space=pltpu.HBM),
+            pl.BlockSpec(memory_space=pltpu.VMEM),
+            pl.BlockSpec(memory_space=pltpu.VMEM),
+            pl.BlockSpec(memory_space=pltpu.VMEM),
+        ),
+        scratch_shapes=[vmem((3, BLOBS, BODIES), F32), vmem((3, BODIES), F32)]
+        + [vmem(x.shape, x.dtype) for x in operands[2:]]
         + [
             vmem((ROWS, BODIES), F32),
             vmem((ROWS, BODIES), F32),
@@ -467,7 +536,8 @@
             vmem((BODIES, 128), F32),
             vmem((128, BODIES), F32),
             vmem((CELLS, BODIES), BF16),
-            vmem((8, BODIES), F32),
+            vmem((8, ROWS), F32),
+            vmem((8, ROWS), F32),
             vmem((PITCH, BODIES), F32),
             vmem((16, BODIES), F32),
             vmem((8, 512), F32),
@@ -476,27 +546,28 @@
             vmem((2, 2, CELLS, CELLS), BF16),
             vmem((2, CELLS, CELLS), BF16),
             vmem((BODIES, ROWS), F32),
+            vmem((RIM, ROWS), F32),
             vmem((3, BLOBS, BODIES), F32),
             vmem((2, RIM, ROWS), F32),
             vmem((2, NEIGH, RIM, ROWS), F32),
-            vmem((3, nx, 8, 256), F32),
-            vmem((3, ny, 8, 256), F32),
-            vmem((3, nz, 8, 256), F32),
+            vmem((3, len(CORE) + 1, 8, 256), F32),
+            vmem((3, len(PLANE) + 1, 8, 256), F32),
+            vmem((3, len(DEPTH) + 1, 8, 256), F32),
             dma((len(operands),)),
             dma(()),
-            dma((2, NEIGH)),
-            dma((2, NEIGH)),
-            dma((3, nx)),
-            dma((3, nx)),
-            dma((3, ny)),
-            dma((3, ny)),
-            dma((3, nz)),
-            dma((3, nz)),
+            dma((2, NEIGH, PARTS)),
+            dma((2, NEIGH, PARTS)),
+            dma((3, len(CORE))),
+            dma((3, len(CORE))),
+            dma((3, len(PLANE))),
+            dma((3, len(PLANE))),
+            dma((3, len(DEPTH))),
+            dma((3, len(DEPTH))),
         ],
-        compiler_params=pltpu.CompilerParams(collective_id=0, has_side_effects=True, vmem_limit_bytes=48 * 2**20),
+        compiler_params=pltpu.CompilerParams(collective_id=0, has_side_effects=True, vmem_limit_bytes=64 * 2**20),
     )(*operands)
-    result = coefs[0, 0] * initial + coefs[1, 0] * u
-    return (result[None, None], coefs[2, 0])
+    result = on_r * initial + on_u * u
+    return (result.reshape(rhs.shape), residual.reshape(()))
 
 
 def solution(mesh):

time: 69.2 us -> 59.9 us (0.87)
  local copies, waits for them, and re-layouts: 8.5 us -> 0.67 us
  Pallas kernels: 58.3 us -> 54.2 us
  between operations: 0.71 us -> 2.35 us
  other arithmetic: 1.38 us -> 2.48 us
    unnamed x25 -> x4, local copies, waits for them, and re-layouts: 7.95 us -> 0.67 us
    pallas_call x1, Pallas kernels: 58.3 us -> 54.2 us  [body(): pl.pallas_call(kernel, out_shape=(jax.ShapeDtypeStruct(initial.shape, F32...]
    unnamed x0 -> x1, other arithmetic: none -> 2.48 us
    broadcast_in_dim x1 -> x0, other arithmetic: 1.38 us -> none  [body(): return (result[None, None], coefs[2, 0])]
where the time goes in v2:
time: 59.9 us; the launch traced here: 59.7 us
  Pallas kernels  54.2 us (90%)
  other arithmetic  2.48 us (4%)
  between operations  2.35 us (4%)
  local copies, waits for them, and re-layouts  0.67 us (1%)
    pallas_call x1, Pallas kernels, body(): pl.pallas_call(kernel, out_shape=(jax.ShapeDtypeStruct(initial.shape, F32...  54.2 us
    unnamed x1, other arithmetic  2.48 us

profile of v2, /device:TPU:1, one launch (start us, length us, event | category | flops | bytes accessed | tf_op | source)
XLA Modules:
  0.0 59.7 jit_solution(16165005021838870671)
XLA Ops:
  0.6 54.2 %shard_map.131 = (f32[3,162,1,256]{3,2,1,0:T(1,128)}, f32[1,256]{1,0:T(1,128)}, f32[1,256]{1,0:T(1,128)}, f32[1,1]{1,0:T(1,128)}) custom-call(f32[3,162,1,256]{3,2,1,0:T(1,128)} %bitcast.14, f32[3,1,256]{2,1,0:T(1,128)} %bitcast.17, f32[486,486]{1,0:T(8,128)} %self_hbm.1, f32[486,486]{1,0:T(8,128)} %near_hbm.1, f32[8,256]{1,0:T(8,128)} %bitcast.15, ...), custom_call_target="tpu_custom_call" | custom-call | tf_op jit(solution)/shard_map/pallas_call | solution.py:511
  54.9 0.0 copy-start.1
  54.9 0.0 copy-start
  54.9 0.6 %copy-done.1 = f32[1,256]{1,0:T(1,128)S(1)} copy-done((f32[1,256]{1,0:T(1,128)S(1)}, f32[1,256]{1,0:T(1,128)}, u32[]{:S(2)}) %copy-start.1) | copy-done | bytes 1048
  55.5 0.0 copy-done
  55.6 2.5 %add_bitcast_fusion = f32[1,1,3,162,256]{4,1,3,2,0:T(1,128)} fusion(f32[3,162,1,256]{3,2,1,0:T(1,128)} %get-tuple-element.8, f32[256]{0:T(256)S(1)} %bitcast.21, f32[256]{0:T(256)S(1)} %bitcast.20, f32[1,1,3,162,256]{4,1,3,2,0:T(1,128)} %param.12), kind=kLoop, calls=%fused_computation | loop fusion | flops 373248 | bytes 1495040
Async XLA Ops:
  54.9 0.6 %copy-start.1 = (f32[1,256]{1,0:T(1,128)S(1)}, f32[1,256]{1,0:T(1,128)}, u32[]{:S(2)}) copy-start(f32[1,256]{1,0:T(1,128)} %get-tuple-element.7) | copy-start | bytes 3076
  54.9 0.7 %copy-start = (f32[1,256]{1,0:T(1,128)S(1)}, f32[1,256]{1,0:T(1,128)}, u32[]{:S(2)}) copy-start(f32[1,256]{1,0:T(1,128)} %get-tuple-element.6) | copy-start | bytes 3076

commit v3 on v2

--- a/solution.py
+++ b/solution.py
@@ -21,6 +21,7 @@
 NN = (((1,), (0,)), ((), ()))
 NT = (((1,), (1,)), ((), ()))
 PARTS = 2
+PLACES = {1: 0, 3: 1, 5: 2, 7: 3, 0: 4, 2: 5, 6: 6, 8: 7}
 
 
 def split(x):
@@ -101,10 +102,10 @@
 
 def kernel(
     rhs_hbm, angles_hbm, self_hbm, near_hbm, weight_hbm, links_hbm, cells_hbm, blob_hbm, perm_hbm, interp_hbm, sibling_hbm, root_hbm,
-    u_hbm, on_r_ref, on_u_ref, residual_ref,
+    result_hbm, residual_ref,
     rhs_in, angles_in, self_in, near_in, weight_in, links_in, cells_in, blob_in, perm_in, interp_in, sibling_in, root_in,
     state_r, state_u, state_t, padded_mat, self_op, near_op, link_op, link_cols, link_rows, occupancy, blob_row, blob_rows, blob_col,
-    rotation, perm_row, square, up_op, sibling_op, root_op, own_gather, self_rim, u_out,
+    rotation, perm_row, square, up_op, down_op, sibling_op, root_op, own_gather, self_rim, u_out,
     rim, halo, stage_c, stage_p, stage_d,
     in_sem, out_sem, rim_send, rim_recv, c_send, c_recv, p_send, p_recv, d_send, d_recv,
 ):
@@ -146,7 +147,14 @@
     beside = {"gy": iy + 1 - 2 * odd}
     far_gx = {"gx": wrapped(ix, 2 * lax.rem(ix, 2) - 1, 8)}
 
+    known = {}
+
     def peer(offset):
+        if offset not in known:
+            known[offset] = device_at(offset)
+        return known[offset]
+
+    def device_at(offset):
         y, core, x, low, high = offset
         device = {}
         if y or core:
@@ -173,6 +181,11 @@
         pending.append(copy)
         return copy
 
+    def drain():
+        for copy in pending:
+            copy.wait_send()
+        pending.clear()
+
     part = RIM // PARTS
 
     def box_copy(phase, source, place, i, device):
@@ -182,22 +195,22 @@
     def start_halo(phase):
         own = rim.at[phase]
         for i in range(PARTS):
-            send(*box_copy(phase, own, 3 + odd, i, beside))
+            send(*box_copy(phase, own, 1 + odd, i, beside))
         for i in range(PARTS):
-            send(*box_copy(phase, own, 4 - odd, i, across))
+            send(*box_copy(phase, own, 2 - odd, i, across))
         for i in range(PARTS):
-            send(*box_copy(phase, own, 1, i, plus))
-            send(*box_copy(phase, own, 6, i, minus))
+            send(*box_copy(phase, own, 0, i, plus))
+            send(*box_copy(phase, own, 3, i, minus))
 
     def forward_halo(phase, place):
         box = halo.at[phase, place]
         for i in range(PARTS):
             remote(*box_copy(phase, rim.at[phase], place, i, plus)).wait_recv()
-            send(*box_copy(phase, box, 2 * (place - 3), i, plus))
-            send(*box_copy(phase, box, 2 * (place - 3) + 5, i, minus))
-
-    def wait_boxes(phase):
-        for place in (1, 6, 0, 5, 2, 7):
+            send(*box_copy(phase, box, place + 3, i, plus))
+            send(*box_copy(phase, box, place + 5, i, minus))
+
+    def wait_boxes(phase, places):
+        for place in places:
             for i in range(PARTS):
                 remote(*box_copy(phase, rim.at[phase], place, i, plus)).wait_recv()
 
@@ -226,18 +239,27 @@
     def start_far(turn, copies, own):
         return start_depth(turn, summed(copies, stage_p, turn) + pltpu.roll(own, 3, axis=0))
 
-    def charges(state):
+    def moments_of(state):
         rows = [
             jnp.sum(blob_col[...] * state[c * PITCH : (c + 1) * PITCH, :], axis=0, keepdims=True) for c in range(3)
         ]
-        moments = jnp.concatenate(rows + [jnp.zeros((5, BODIES), F32)], axis=0)
+        return jnp.concatenate(rows + [jnp.zeros((5, BODIES), F32)], axis=0)
+
+    def charges(moments):
         return fold(mm(stacked(moments), occupancy[...], NT))
+
+    low_bit = lax.rem(iz, 2) == 1
+    high_bit = iz // 2 == 1
+
+    def pick(flag, a, b):
+        return jnp.where(flag, a, b)
+
+    def pair(ref):
+        return (ref[0], ref[1])
 
     def far_values(turn, copies):
         for copy in copies:
             copy.wait_recv()
-        low_bit = lax.rem(iz, 2) == 1
-        high_bit = iz // 2 == 1
         top = iota((8, CELLS), 0) < 3
         layers = []
         for high in range(4):
@@ -245,7 +267,6 @@
             there = stage_d[turn, DEPTH.index((0, 0, 0, 1, high)) + 1]
             layers.append(jnp.where(top, here + there - pltpu.roll(here, 5, axis=0), here))
         own, one, two, three = layers
-        pick = lambda flag, a, b: jnp.where(flag, a, b)
         joined = jnp.concatenate(
             [
                 jnp.concatenate([pick(low_bit, one, own), pick(low_bit, own, one)], axis=1),
@@ -253,20 +274,12 @@
             ],
             axis=0,
         )
-        up = [(up_op[0, level], up_op[1, level]) for level in range(2)]
-        siblings = [(sibling_op[0, level], sibling_op[1, level]) for level in range(2)]
-        first = mm_few(joined, up[0])
+        first = mm_few(joined, pair(up_op))
         mine, partner = first[:8], first[8:]
         second = jnp.concatenate([pick(high_bit, partner, mine), pick(high_bit, mine, partner)], axis=1)
-        others = mm_few(second, up[1])
-        potential = mm_few(others, (root_op[0], root_op[1]))
-        placed = mm_few(potential, up[1], NT)
-        potential = pick(high_bit, placed[:, CELLS:], placed[:, :CELLS])
-        potential = potential + pltpu.roll(mm_few(partner, siblings[1]), 5, axis=0)
-        placed = mm_few(potential, up[0], NT)
-        potential = pick(low_bit, placed[:, CELLS:], placed[:, :CELLS])
-        potential = potential + pltpu.roll(mm_few(one, siblings[0]), 5, axis=0)
-        return fold(mm(stacked(potential), occupancy[...]))
+        potential = mm_few(second, pair(root_op)) + pltpu.roll(mm_few(partner, pair(sibling_op.at[1])), 5, axis=0)
+        potential = mm_few(potential, pair(down_op), NT) + pltpu.roll(mm_few(one, pair(sibling_op.at[0])), 5, axis=0)
+        return jnp.where(top, fold(mm(stacked(potential), occupancy[...])), 0.0)
 
     def factor(target, source, inverse):
         index = 3 * source + target if inverse else 3 * target + source
@@ -290,17 +303,12 @@
     def write_own_gather(state):
         own_gather[...] = mm3((link_op[0, :, :BODIES], link_op[1, :, :BODIES]), split(state[...]), NT)
 
-    def boxes_of(phase):
-        return split(halo[phase].reshape(NEIGH * RIM, ROWS))
-
-    def gathered(bodies, boxes):
-        return own_gather[:bodies, :] + mm3((link_op[0, :bodies, BODIES:], link_op[1, :bodies, BODIES:]), boxes)
-
-    def near_pair():
-        return (near_op[0], near_op[1])
-
-    def finish(result, boxes, values):
-        result[...] += mm3(near_pair(), split(gathered(BODIES, boxes)), NT)
+    def add_boxes(phase, first, last):
+        lanes = slice(BODIES + first * RIM, BODIES + last * RIM)
+        boxes = split(halo[phase, first:last].reshape((last - first) * RIM, ROWS))
+        return own_gather[...] + mm3((link_op[0, :, lanes], link_op[1, :, lanes]), boxes)
+
+    def add_far(result, values):
         for c in range(3):
             result[c * PITCH : (c + 1) * PITCH, :] += blob_col[...] * values[c : c + 1, :]
 
@@ -320,6 +328,31 @@
     for c in range(3):
         state_r[body_rows(c), :] = rhs_in[c]
     rim[0] = state_r[:, :128].T[:RIM]
+    loads["weight"].wait()
+    loads["links"].wait()
+    links = links_in[...]
+    box, body = links // BODIES, lax.rem(links, BODIES)
+    place = jnp.zeros_like(box)
+    for slot, index in PLACES.items():
+        place = jnp.where(box == slot, index, place)
+    lane_of = jnp.where(box == 4, body, BODIES + place * RIM + body)
+    link_rows[...] = jnp.zeros_like(link_rows)
+    link_rows[0:NEIGH, :] = lane_of.astype(F32)
+    link_rows[NEIGH : 2 * NEIGH, :] = weight_in[...]
+    link_cols[...] = link_rows[...].T
+    block = 32
+
+    @pl.loop(0, BODIES // block)
+    def _(i):
+        rows = pl.ds(pl.multiple_of(i * block, block), block)
+        entries = link_cols[rows, :]
+        width = BODIES + NEIGH * RIM
+        lane = iota((block, width), 1).astype(F32)
+        weights = jnp.zeros((block, width), F32)
+        for k in range(NEIGH):
+            weights = weights + jnp.where(lane == entries[:, k : k + 1], entries[:, NEIGH + k : NEIGH + k + 1], 0.0)
+        link_op[0, rows, :], link_op[1, rows, :] = split(weights)
+
     pl.semaphore_wait(barrier, len(greeted))
     start_halo(0)
 
@@ -328,10 +361,11 @@
     blob_row[...] = jnp.zeros_like(blob_row)
     blob_row[0:1, :BLOBS] = blob_in[...]
     diagonal = iota((PITCH, BODIES), 0) == iota((PITCH, BODIES), 1)
+    blob_square = total(blob_row[0:1, :] * blob_row[0:1, :])
     column = jnp.sum(jnp.where(diagonal, blob_row[0:1, :BODIES], 0.0), axis=1, keepdims=True)
     blob_col[...] = jnp.broadcast_to(column, (PITCH, BODIES))
     occupancy[...] = jnp.where(iota((CELLS, BODIES), 0) == cells_in[...], 1.0, 0.0).astype(BF16)
-    own_charges = charges(state_r)
+    own_charges = charges(moments_of(state_r))
     copies = start_core(0, own_charges)
 
     loads["angles"].wait()
@@ -346,6 +380,7 @@
         loads[name].wait()
     lane_few = iota((8, 512), 1)
     blob_first = blob_row[...]
+    blob_rows[...] = jnp.zeros_like(blob_rows)
     for c in range(3):
         blob_rows[c : c + 1, :] = pltpu.roll(blob_first, c * PITCH, axis=1)[0:1] if c else blob_first[0:1]
     perm_row[...] = jnp.full_like(perm_row, -1.0)
@@ -356,83 +391,73 @@
     kept_rows = jnp.where(lane_few < SKEL, perm_all, -1.0)[:, :CELLS]
     rest_rows = jnp.where(lane_few < SKEL, pltpu.roll(perm_all, 512 - SKEL, axis=1), -1.0)[:, :CELLS]
     square[...] = jnp.zeros_like(square)
+    place = iota((2 * CELLS, CELLS), 0).astype(F32)
+    ups = []
     for level in range(2):
-        place = iota((2 * CELLS, CELLS), 0).astype(F32)
         kept = jnp.where(place == kept_rows[level : level + 1], 1.0, 0.0)
         rest = jnp.where(place == rest_rows[level : level + 1], 1.0, 0.0).astype(BF16)
         square[:SKEL, :SKEL] = interp_in[level]
         high, low = split(square[...])
-        up_op[0, level], up_op[1, level] = split(kept + (mm(rest, high) + mm(rest, low)))
+        ups.append(kept + (mm(rest, high) + mm(rest, low)))
         square[:SKEL, :SKEL] = sibling_in[level]
-        sibling_op[0, level], sibling_op[1, level] = split(square[...])
+        sibling_op[level, 0], sibling_op[level, 1] = split(square[...])
+    up_op[0], up_op[1] = split(ups[0])
+    down_op[0], down_op[1] = split(pick(low_bit, ups[0][CELLS:], ups[0][:CELLS]))
     square[:SKEL, :SKEL] = root_in[...]
-    root_op[0], root_op[1] = split(square[...])
-
-    forward_halo(0, 4 - odd)
+    below = mm3(split(square[...]), split(pick(high_bit, ups[1][CELLS:], ups[1][:CELLS])), NT)
+    root_op[0], root_op[1] = split(mm3(split(ups[1]), split(below)))
+
+    forward_halo(0, 2 - odd)
     copies = start_far(0, copies, own_charges)
     write_self(state_r, state_u)
-    self_rim[...] = state_u[:, :128].T[:RIM]
-    forward_halo(0, 3 + odd)
-
-    loads["weight"].wait()
-    loads["links"].wait()
-    links = links_in[...]
-    box, body = links // BODIES, lax.rem(links, BODIES)
-    place = jnp.where(box < 4, box, box - 1)
-    lane_of = jnp.where(box == 4, body, BODIES + place * RIM + body)
-    link_rows[...] = jnp.zeros_like(link_rows)
-    link_rows[0:NEIGH, :] = lane_of.astype(F32)
-    link_rows[NEIGH : 2 * NEIGH, :] = weight_in[...]
-    link_cols[...] = link_rows[...].T
-    block = 32
-
-    @pl.loop(0, BODIES // block)
-    def _(i):
-        rows = pl.ds(pl.multiple_of(i * block, block), block)
-        entries = link_cols[rows, :]
-        width = BODIES + NEIGH * RIM
-        lane = iota((block, width), 1).astype(F32)
-        weights = jnp.zeros((block, width), F32)
-        for k in range(NEIGH):
-            weights = weights + jnp.where(lane == entries[:, k : k + 1], entries[:, NEIGH + k : NEIGH + k + 1], 0.0)
-        link_op[0, rows, :], link_op[1, rows, :] = split(weights)
+    forward_halo(0, 1 + odd)
 
     loads["near"].wait()
     write_operator(near_in, near_op)
     write_own_gather(state_r)
+    wait_boxes(0, (0, 3))
+    own_gather[...] = add_boxes(0, 0, 4)
+    near = pair(near_op)
+    near_moments = stacked(mm_few(blob_rows[...], near))
+    self_moments = moments_of(state_u)
+    self_rim[...] = state_u[:, :128].T[:RIM]
     values = far_values(0, copies)
-    wait_boxes(0)
-
-    boxes = boxes_of(0)
     columns = jnp.concatenate([values, jnp.zeros((120, BODIES), F32)], axis=0)[:, :128].T[:RIM]
-    far_rim = sum(columns[:, c : c + 1] * blob_rows[c : c + 1, :] for c in range(3))
-    rim[1] = self_rim[...] + mm3(split(gathered(RIM, boxes)), near_pair(), NT) + far_rim
+    self_rim[...] += sum(columns[:, c : c + 1] * blob_rows[c : c + 1, :] for c in range(3))
+    add_far(state_u, values)
+    drain()
+    wait_boxes(0, (4, 5, 6, 7))
+
+    high, low = split(add_boxes(0, 4, 8))
+    rim[1] = self_rim[...] + mm3((high[:RIM], low[:RIM]), near, NT)
     start_halo(1)
-    finish(state_u, boxes, values)
-    own_charges = charges(state_u)
+    moments = self_moments + blob_square * values + fold(mm(near_moments, high, NT) + mm(near_moments, low, NT))
+    own_charges = charges(moments)
     copies = start_core(1, own_charges)
+    state_u[...] += mm3(near, (high, low), NT)
+    copies = start_plane(1, summed(copies, stage_c, 1))
+    write_self(state_u, state_t)
+    write_own_gather(state_u)
+    forward_halo(1, 2 - odd)
     for c in range(3):
         u_out[c] = state_u[body_rows(c), :]
-    store = pltpu.make_async_copy(u_out, u_hbm.at[:, :, 0, :], out_sem)
-    store.start()
-    write_self(state_u, state_t)
-    copies = start_plane(1, summed(copies, stage_c, 1))
-    forward_halo(1, 4 - odd)
-    write_own_gather(state_u)
 
     tiny = 1e-30
     rr = total(state_r[...] * state_r[...])
     ru = total(state_r[...] * state_u[...])
     over_rr = jnp.where(rr > 0.0, 1.0 / jnp.where(rr > 0.0, rr, 1.0), 0.0)
-    forward_halo(1, 3 + odd)
+    forward_halo(1, 1 + odd)
+    copies = start_far(1, copies, own_charges)
     state_u[...] = state_u[...] - (ru * over_rr) * state_r[...]
     uu = total(state_u[...] * state_u[...])
     over_uu = jnp.where(uu > 0.0, 1.0 / jnp.where(uu > 0.0, uu, 1.0), 0.0)
-
-    copies = start_far(1, copies, own_charges)
-    values = far_values(1, copies)
-    wait_boxes(1)
-    finish(state_t, boxes_of(1), values)
+    wait_boxes(1, (0, 3))
+    own_gather[...] = add_boxes(1, 0, 4)
+    drain()
+
+    add_far(state_t, far_values(1, copies))
+    wait_boxes(1, (4, 5, 6, 7))
+    state_t[...] += mm3(near, split(add_boxes(1, 4, 8)), NT)
 
     largest = jnp.maximum(jnp.max(jnp.abs(state_t[...]), axis=(0, 1), keepdims=True), tiny)
     scaled = state_t[...] * (1.0 / largest)
@@ -458,6 +483,7 @@
     copies = start_core(2, tile)
     copies = start_plane(2, summed(copies, stage_c, 2))
     copies = start_depth(2, summed(copies, stage_p, 2))
+    drain()
     everyone = summed(copies, stage_d, 2)
 
     r1, u1, u2, t1, t2, t3 = (everyone[i : i + 1] for i in range(6))
@@ -481,13 +507,13 @@
     coef_one, coef_two, residual = least_squares(beta, diag_first, below_first, above_second, diag_second, below_second)
     on_r = coef_one / beta + coef_two * rest / below_first
     on_u = coef_two / (below_first * beta)
-    on_r_ref[...] = jnp.broadcast_to(on_r, (1, BODIES))
-    on_u_ref[...] = jnp.broadcast_to(on_u, (1, BODIES))
+    for c in range(3):
+        u_out[c] = on_r * rhs_in[c] + on_u * u_out[c]
+    store = pltpu.make_async_copy(u_out, result_hbm.at[:, :, 0, :], out_sem)
+    store.start()
     residual_ref[...] = residual
 
     store.wait()
-    for copy in pending:
-        copy.wait_send()
 
 
 def body(rhs, angles, self_mob, near_mat, near_weight, neighbours, cells, blob_weight, skel_perm, interp, sibling_ops, root_op):
@@ -508,19 +534,15 @@
     ]
     vmem = pltpu.VMEM
     dma = pltpu.SemaphoreType.DMA
-    u, on_r, on_u, residual = pl.pallas_call(
+    result, residual = pl.pallas_call(
         kernel,
         out_shape=(
             jax.ShapeDtypeStruct(initial.shape, F32),
-            jax.ShapeDtypeStruct((1, BODIES), F32),
-            jax.ShapeDtypeStruct((1, BODIES), F32),
             jax.ShapeDtypeStruct((1, 1), F32),
         ),
         in_specs=[pl.BlockSpec(memory_space=pltpu.HBM)] * len(operands),
         out_specs=(
             pl.BlockSpec(memory_space=pltpu.HBM),
-            pl.BlockSpec(memory_space=pltpu.VMEM),
-            pl.BlockSpec(memory_space=pltpu.VMEM),
             pl.BlockSpec(memory_space=pltpu.VMEM),
         ),
         scratch_shapes=[vmem((3, BLOBS, BODIES), F32), vmem((3, BODIES), F32)]
@@ -542,9 +564,10 @@
             vmem((16, BODIES), F32),
             vmem((8, 512), F32),
             vmem((CELLS, CELLS), F32),
-            vmem((2, 2, 2 * CELLS, CELLS), BF16),
+            vmem((2, 2 * CELLS, CELLS), BF16),
+            vmem((2, CELLS, CELLS), BF16),
             vmem((2, 2, CELLS, CELLS), BF16),
-            vmem((2, CELLS, CELLS), BF16),
+            vmem((2, 2 * CELLS, CELLS), BF16),
             vmem((BODIES, ROWS), F32),
             vmem((RIM, ROWS), F32),
             vmem((3, BLOBS, BODIES), F32),
@@ -566,7 +589,6 @@
         ],
         compiler_params=pltpu.CompilerParams(collective_id=0, has_side_effects=True, vmem_limit_bytes=64 * 2**20),
     )(*operands)
-    result = on_r * initial + on_u * u
     return (result.reshape(rhs.shape), residual.reshape(()))
 
 

time: 59.9 us -> 57.6 us (0.962)
  other arithmetic: 2.48 us -> 0 us
  local copies, waits for them, and re-layouts: 0.67 us -> 2.15 us
  Pallas kernels: 54.2 us -> 52.8 us
    unnamed x1 -> x0, other arithmetic: 2.48 us -> none
    unnamed x4 -> x1, local copies, waits for them, and re-layouts: 0.67 us -> 2.15 us
    pallas_call x1, Pallas kernels: 54.2 us -> 52.8 us  [body(): pl.pallas_call(kernel, out_shape=(jax.ShapeDtypeStruct(initial.shape, F32...]
where the time goes in v3:
time: 57.6 us; the launch traced here: 57.4 us
  Pallas kernels  52.8 us (92%)
  between operations  2.46 us (4%)
  local copies, waits for them, and re-layouts  2.15 us (4%)
    pallas_call x1, Pallas kernels, body(): pl.pallas_call(kernel, out_shape=(jax.ShapeDtypeStruct(initial.shape, F32...  52.8 us
    unnamed x1, local copies, waits for them, and re-layouts  2.15 us

profile of v3, /device:TPU:1, one launch (start us, length us, event | category | flops | bytes accessed | tf_op | source)
XLA Modules:
  0.0 57.4 jit_solution(15709786224335248913)
XLA Ops:
  0.6 52.8 %shard_map.131 = (f32[3,162,1,256]{3,2,1,0:T(1,128)}, f32[1,1]{1,0:T(1,128)}) custom-call(f32[3,162,1,256]{3,2,1,0:T(1,128)} %bitcast.10, f32[3,1,256]{2,1,0:T(1,128)} %bitcast.14, f32[486,486]{1,0:T(8,128)} %self_hbm.1, f32[486,486]{1,0:T(8,128)} %near_hbm.1, f32[8,256]{1,0:T(8,128)} %bitcast.12, s32[8,256]{1,0:T(8,128)} %bitcast.13, s32[1,256]{1,0:T(1,128)} %bitcast.15, ...), custom_call_target="tpu_custom_call" | custom-call | tf_op jit(solution)/shard_map/pallas_call | solution.py:537
  53.4 2.2 %copy.17 = f32[1,1,3,162,256]{4,1,3,2,0:T(1,128)} copy(f32[1,1,3,162,256]{4,1,3,2,0:T(1,128)} %bitcast.11) | data formatting | bytes 995328

commit v4 on v3

--- a/solution.py
+++ b/solution.py
@@ -121,7 +121,8 @@
     for c in range(3):
         state_r[pad_rows(c), :] = jnp.zeros_like(state_r[pad_rows(c), :])
     pairs = {
-        "rhs": (rhs_hbm.at[:, :, 0, :], rhs_in),
+        "rhs": (rhs_hbm.at[:, :, 0, :128], rhs_in.at[:, :, :128]),
+        "rest": (rhs_hbm.at[:, :, 0, 128:], rhs_in.at[:, :, 128:]),
         "blob": (blob_hbm, blob_in),
         "cells": (cells_hbm, cells_in),
         "angles": (angles_hbm.at[:, 0, :], angles_in),
@@ -135,8 +136,7 @@
         "near": (near_hbm, near_in),
     }
     loads = {name: pltpu.make_async_copy(a, b, in_sem.at[i]) for i, (name, (a, b)) in enumerate(pairs.items())}
-    for load in loads.values():
-        load.start()
+    loads["rhs"].start()
 
     def wrapped(index, shift, size):
         return lax.rem(index + shift + size, size)
@@ -169,6 +169,9 @@
     greeted = [across, far_gx] + [peer(o) for o in sorted(DEPTH + PLANE + CORE, key=hops, reverse=True)]
     for device in greeted:
         pl.semaphore_signal(barrier, inc=1, device_id=device, device_id_type=MESH)
+    for name, load in loads.items():
+        if name != "rhs":
+            load.start()
 
     def remote(src, dst, send_sem, recv_sem, device):
         return pltpu.make_async_remote_copy(
@@ -222,6 +225,13 @@
         ]
         return copies[::-1]
 
+    def packed(x):
+        return x[:, :128] + pltpu.roll(x[:, 128:], 3, axis=0)
+
+    def unpacked(x):
+        top = iota((8, 128), 0) < 3
+        return jnp.concatenate([jnp.where(top, x, 0.0), jnp.where(top, pltpu.roll(x, 5, axis=0), 0.0)], axis=1)
+
     def start_core(turn, value):
         return exchange(stage_c, c_send, c_recv, CORE, turn, value)
 
@@ -237,7 +247,7 @@
         return jnp.sum(stage[turn], axis=0)
 
     def start_far(turn, copies, own):
-        return start_depth(turn, summed(copies, stage_p, turn) + pltpu.roll(own, 3, axis=0))
+        return start_depth(turn, unpacked(summed(copies, stage_p, turn)) + pltpu.roll(own, 3, axis=0))
 
     def moments_of(state):
         rows = [
@@ -326,8 +336,11 @@
 
     loads["rhs"].wait()
     for c in range(3):
-        state_r[body_rows(c), :] = rhs_in[c]
+        state_r[body_rows(c), :128] = rhs_in[c, :, :128]
     rim[0] = state_r[:, :128].T[:RIM]
+    loads["rest"].wait()
+    for c in range(3):
+        state_r[body_rows(c), 128:] = rhs_in[c, :, 128:]
     loads["weight"].wait()
     loads["links"].wait()
     links = links_in[...]
@@ -366,7 +379,7 @@
     blob_col[...] = jnp.broadcast_to(column, (PITCH, BODIES))
     occupancy[...] = jnp.where(iota((CELLS, BODIES), 0) == cells_in[...], 1.0, 0.0).astype(BF16)
     own_charges = charges(moments_of(state_r))
-    copies = start_core(0, own_charges)
+    copies = start_core(0, packed(own_charges))
 
     loads["angles"].wait()
     for target, row in enumerate(frame(angles_in[...])):
@@ -429,11 +442,11 @@
     wait_boxes(0, (4, 5, 6, 7))
 
     high, low = split(add_boxes(0, 4, 8))
+    moments = self_moments + blob_square * values + fold(mm(near_moments, high, NT) + mm(near_moments, low, NT))
+    own_charges = charges(moments)
+    copies = start_core(1, packed(own_charges))
     rim[1] = self_rim[...] + mm3((high[:RIM], low[:RIM]), near, NT)
     start_halo(1)
-    moments = self_moments + blob_square * values + fold(mm(near_moments, high, NT) + mm(near_moments, low, NT))
-    own_charges = charges(moments)
-    copies = start_core(1, own_charges)
     state_u[...] += mm3(near, (high, low), NT)
     copies = start_plane(1, summed(copies, stage_c, 1))
     write_self(state_u, state_t)
@@ -446,8 +459,8 @@
     rr = total(state_r[...] * state_r[...])
     ru = total(state_r[...] * state_u[...])
     over_rr = jnp.where(rr > 0.0, 1.0 / jnp.where(rr > 0.0, rr, 1.0), 0.0)
+    copies = start_far(1, copies, own_charges)
     forward_halo(1, 1 + odd)
-    copies = start_far(1, copies, own_charges)
     state_u[...] = state_u[...] - (ru * over_rr) * state_r[...]
     uu = total(state_u[...] * state_u[...])
     over_uu = jnp.where(uu > 0.0, 1.0 / jnp.where(uu > 0.0, uu, 1.0), 0.0)
@@ -475,14 +488,16 @@
         largest * (ut * over_uu * root_uu),
         largest * jnp.sqrt(tt),
     ]
-    row_of = iota((8, 256), 0)
-    lane_is_mine = iota((8, 256), 1) == ix + 8 * (iy + 8 * iz)
-    tile = jnp.zeros((8, 256), F32)
+    height = 2 * iz + odd
+    row_of = iota((8, 128), 0)
+    lane_is_mine = iota((8, 128), 1) == 4 * ix + iy // 2 + 32 * lax.rem(height, 4)
+    tile = jnp.zeros((8, 128), F32)
     for i, value in enumerate(triangle):
         tile = jnp.where((row_of == i) & lane_is_mine, value, tile)
     copies = start_core(2, tile)
     copies = start_plane(2, summed(copies, stage_c, 2))
-    copies = start_depth(2, summed(copies, stage_p, 2))
+    tile = summed(copies, stage_p, 2)
+    copies = start_depth(2, jnp.concatenate([jnp.where(height < 4, tile, 0.0), jnp.where(height < 4, 0.0, tile)], axis=1))
     drain()
     everyone = summed(copies, stage_d, 2)
 
@@ -573,10 +588,10 @@
             vmem((3, BLOBS, BODIES), F32),
             vmem((2, RIM, ROWS), F32),
             vmem((2, NEIGH, RIM, ROWS), F32),
-            vmem((3, len(CORE) + 1, 8, 256), F32),
-            vmem((3, len(PLANE) + 1, 8, 256), F32),
+            vmem((3, len(CORE) + 1, 8, 128), F32),
+            vmem((3, len(PLANE) + 1, 8, 128), F32),
             vmem((3, len(DEPTH) + 1, 8, 256), F32),
-            dma((len(operands),)),
+            dma((len(operands) + 1,)),
             dma(()),
             dma((2, NEIGH, PARTS)),
             dma((2, NEIGH, PARTS)),

time: 57.6 us -> 55 us (0.955)
  Pallas kernels: 52.8 us -> 50.1 us
    pallas_call x1, Pallas kernels: 52.8 us -> 50.1 us  [body(): pl.pallas_call(kernel, out_shape=(jax.ShapeDtypeStruct(initial.shape, F32...]
where the time goes in v4:
time: 55 us; the launch traced here: 54.7 us
  Pallas kernels  50.1 us (91%)
  between operations  2.46 us (4%)
  local copies, waits for them, and re-layouts  2.15 us (4%)
    pallas_call x1, Pallas kernels, body(): pl.pallas_call(kernel, out_shape=(jax.ShapeDtypeStruct(initial.shape, F32...  50.1 us
    unnamed x1, local copies, waits for them, and re-layouts  2.15 us

profile of v4, /device:TPU:1, one launch (start us, length us, event | category | flops | bytes accessed | tf_op | source)
XLA Modules:
  0.0 54.7 jit_solution(8105680704973362860)
XLA Ops:
  0.6 50.1 %shard_map.131 = (f32[3,162,1,256]{3,2,1,0:T(1,128)}, f32[1,1]{1,0:T(1,128)}) custom-call(f32[3,162,1,256]{3,2,1,0:T(1,128)} %bitcast.10, f32[3,1,256]{2,1,0:T(1,128)} %bitcast.14, f32[486,486]{1,0:T(8,128)} %self_hbm.1, f32[486,486]{1,0:T(8,128)} %near_hbm.1, f32[8,256]{1,0:T(8,128)} %bitcast.12, s32[8,256]{1,0:T(8,128)} %bitcast.13, s32[1,256]{1,0:T(1,128)} %bitcast.15, ...), custom_call_target="tpu_custom_call" | custom-call | tf_op jit(solution)/shard_map/pallas_call | solution.py:552
  50.8 2.2 %copy.17 = f32[1,1,3,162,256]{4,1,3,2,0:T(1,128)} copy(f32[1,1,3,162,256]{4,1,3,2,0:T(1,128)} %bitcast.11) | data formatting | bytes 995328

commit v5 on v4

--- a/solution.py
+++ b/solution.py
@@ -200,10 +200,10 @@
         for i in range(PARTS):
             send(*box_copy(phase, own, 1 + odd, i, beside))
         for i in range(PARTS):
-            send(*box_copy(phase, own, 2 - odd, i, across))
-        for i in range(PARTS):
             send(*box_copy(phase, own, 0, i, plus))
             send(*box_copy(phase, own, 3, i, minus))
+        for i in range(PARTS):
+            send(*box_copy(phase, own, 2 - odd, i, across))
 
     def forward_halo(phase, place):
         box = halo.at[phase, place]

time: 55 us -> 55 us (level)
  no operation moved by 1% of the time
where the time goes in v5:
time: 55 us; the launch traced here: 54.7 us
  Pallas kernels  50.1 us (91%)
  between operations  2.46 us (4%)
  local copies, waits for them, and re-layouts  2.15 us (4%)
    pallas_call x1, Pallas kernels, body(): pl.pallas_call(kernel, out_shape=(jax.ShapeDtypeStruct(initial.shape, F32...  50.1 us
    unnamed x1, local copies, waits for them, and re-layouts  2.15 us

profile of v5, /device:TPU:1, one launch (start us, length us, event | category | flops | bytes accessed | tf_op | source)
XLA Modules:
  0.0 54.7 jit_solution(7339028956280605357)
XLA Ops:
  0.6 50.1 %shard_map.131 = (f32[3,162,1,256]{3,2,1,0:T(1,128)}, f32[1,1]{1,0:T(1,128)}) custom-call(f32[3,162,1,256]{3,2,1,0:T(1,128)} %bitcast.10, f32[3,1,256]{2,1,0:T(1,128)} %bitcast.14, f32[486,486]{1,0:T(8,128)} %self_hbm.1, f32[486,486]{1,0:T(8,128)} %near_hbm.1, f32[8,256]{1,0:T(8,128)} %bitcast.12, s32[8,256]{1,0:T(8,128)} %bitcast.13, s32[1,256]{1,0:T(1,128)} %bitcast.15, ...), custom_call_target="tpu_custom_call" | custom-call | tf_op jit(solution)/shard_map/pallas_call | solution.py:552
  50.8 2.2 %copy.17 = f32[1,1,3,162,256]{4,1,3,2,0:T(1,128)} copy(f32[1,1,3,162,256]{4,1,3,2,0:T(1,128)} %bitcast.11) | data formatting | bytes 995328
